TPU v7x, 512 devices: a whole 4x4x16 slice. The times are simulated.
512 devices in a mesh: slab: 16 (over z_lo, core), src: 32 (over y, x, z_hi).
Axes of the slice: x: 4, y: 4, z: 16 (z_hi: 2, z_lo: 8; z = z_hi * 8 + z_lo), core: 2. Of those that a mesh axis runs over, the one named last changes fastest.
Arguments:
- trace_values: bfloat16 [32, 8192, 128], P('src', 'slab'), may hold values from -6 to 6
- trace_owner: int32 [32, 8192, 1], P('src', 'slab'), may hold values from 0 to 15; in each aligned block of 512 rows (0 to 511, 512 to 1023, ..., all dimensions but the last counted through in order) at most 64 rows name the same one
- trace_source: int32 [32, 8192], P('src', 'slab'), may hold values from 0 to 511
- source_fields: bfloat16 [2, 8192, 16384], P(None, 'slab', 'src'), may hold values from -0.03125 to 0.03125
- green_fields: bfloat16 [2, 2048, 16384], P(None, 'slab', 'src'), may hold values from -0.0625 to 0.0625
Outputs:
- gradient: float32 [16384], P('src')
Inputs may be any that keep to these rules, and one draw needn't show every extreme that they name: `trace_owner`: among the traces of one device, no owner is named by more than 64 traces, a bound that some block reaches.
All inputs are finite; a program needn't handle non-finite values.
Results may differ from a plain program's by a relative error of at most 0.0026.
Values may be sent and summed in bfloat16 or wider, within the bound.
A program may use at most 64 MiB of HBM per device.

v0:
```python
import jax
import jax.numpy as jnp
from jax import lax
from jax.sharding import PartitionSpec as P


def on_device(trace_values, trace_owner, trace_source, source_fields, green_fields):
    values = trace_values[0]
    owners = trace_owner[0, :, 0]
    locals_id = trace_source[0]
    trace_count = values.shape[0]
    width = values.shape[1]
    half_width = width // 2
    slab_count = lax.axis_size("slab")
    src_count = lax.axis_size("src")
    sources_here = source_fields.shape[1]
    source_ids = jnp.arange(sources_here, dtype=jnp.int32)
    iota_high = (source_ids // 32).astype(jnp.bfloat16)
    iota_low = (source_ids % 32).astype(jnp.bfloat16)
    capacity = 2 * trace_count // slab_count
    owner_hits = (owners[:, None] == jnp.arange(slab_count, dtype=jnp.int32)[None, :]).astype(
        jnp.int32
    )
    ranks = jnp.sum(jnp.cumsum(owner_hits, axis=0) * owner_hits, axis=1) - 1
    slots = owners * capacity + ranks
    placing = (
        jnp.arange(slab_count * capacity, dtype=jnp.int32)[:, None] == slots[None, :]
    ).astype(jnp.bfloat16)
    sent_values = jnp.dot(placing, values, preferred_element_type=jnp.float32).astype(jnp.bfloat16)
    labels = jnp.stack([locals_id // 32 + 1, locals_id % 32 + 1], axis=1).astype(jnp.bfloat16)
    sent_labels = (jnp.dot(placing, labels, preferred_element_type=jnp.float32) - 1.0).astype(
        jnp.bfloat16
    )
    got_values, got_labels = (
        lax.all_to_all(
            sent_values.reshape(slab_count, capacity, width),
            "slab",
            split_axis=0,
            concat_axis=0,
            tiled=True,
        ),
        lax.all_to_all(
            sent_labels.reshape(slab_count, capacity, 2),
            "slab",
            split_axis=0,
            concat_axis=0,
            tiled=True,
        ),
    )
    flat_labels = got_labels.reshape(-1, 2)
    picks = (
        (iota_high[:, None] == flat_labels[None, :, 0])
        & (iota_low[:, None] == flat_labels[None, :, 1])
    ).astype(jnp.bfloat16)
    assembled = jnp.dot(picks, got_values.reshape(-1, width), preferred_element_type=jnp.float32)
    residual_piece = assembled.astype(jnp.bfloat16)
    residual_rows = lax.all_gather(residual_piece, "src", axis=1, tiled=True)
    split_rows = residual_rows.reshape(sources_here, src_count, 2, half_width)
    res_real = split_rows[:, :, 0, :].reshape(sources_here, src_count * half_width)
    res_imag = split_rows[:, :, 1, :].reshape(sources_here, src_count * half_width)
    piece = lax.all_gather(green_fields, "slab", axis=1, tiled=True)
    adj_real = jnp.dot(res_real, piece[0], preferred_element_type=jnp.float32) + jnp.dot(
        res_imag, piece[1], preferred_element_type=jnp.float32
    )
    adj_imag = jnp.dot(res_real, piece[1], preferred_element_type=jnp.float32) - jnp.dot(
        res_imag, piece[0], preferred_element_type=jnp.float32
    )
    adj_real, adj_imag = (adj_real, adj_imag)
    partial_value = jnp.sum(
        source_fields[0].astype(jnp.float32) * adj_real
        - source_fields[1].astype(jnp.float32) * adj_imag,
        axis=0,
    )
    return lax.psum(partial_value, "slab")


def solution(mesh):
    in_specs = (
        P("src", "slab", None),
        P("src", "slab", None),
        P("src", "slab"),
        P(None, "slab", "src"),
        P(None, "slab", "src"),
    )
    out_specs = P("src")
    return jax.shard_map(
        on_device, mesh=mesh, in_specs=in_specs, out_specs=out_specs, check_vma=False
    )
```

profile of v0, /device:TPU:1, one launch (start us, length us, event | category | flops | bytes accessed | tf_op | source)
XLA Modules:
  0.0 426.7 jit_solution(941762704033851159)
XLA Ops:
  6.5 0.0 copy-start
  6.5 0.7 fusion.31
  7.3 1.1 reduce-window.6
  8.4 0.2 slice_reduce_fusion
  8.7 0.8 fusion.30
  9.4 0.7 add_add_fusion
  10.1 0.7 add_convert_fusion
  10.8 0.5 fusion.21
  11.3 0.1 reshape.180
  11.4 0.6 copy.12
  12.0 14.0 %all-to-all-start = ((bf16[16,64,2]{1,2,0:T(2,128)(2,1)}), bf16[16,64,2]{1,2,0:T(2,128)(2,1)S(1)}, u32[]{:S(2)}, u32[]{:S(2)}) async-start(bf16[16,64,2]{1,2,0:T(2,128)(2,1)} %copy.12), calls=%async_computation | async-start | bytes 16384 | tf_op jit(solution)/shard_map/all_to_all | solution.py:42
  26.0 0.0 copy-done
  26.0 1.2 fusion.16
  27.2 8.6 %all-to-all-done = bf16[16,64,2]{1,2,0:T(2,128)(2,1)S(1)} async-done(((bf16[16,64,2]{1,2,0:T(2,128)(2,1)}), bf16[16,64,2]{1,2,0:T(2,128)(2,1)S(1)}, u32[]{:S(2)}, u32[]{:S(2)}) %all-to-all-start) | async-done | bytes 4128 | tf_op jit(solution)/shard_map/all_to_all | solution.py:42
  35.7 4.0 all-to-all-start.1
  39.8 0.0 all-gather.3.cloned.1.call-start
  39.9 0.1 reshape.181
  40.0 16.9 %all-to-all-done.1 = bf16[16,64,128]{2,1,0:T(8,128)(2,1)S(1)} async-done(((bf16[16,64,128]{2,1,0:T(8,128)(2,1)}), bf16[16,64,128]{2,1,0:T(8,128)(2,1)S(1)}, u32[]{:S(2)}, u32[]{:S(2)}) %all-to-all-start.1) | async-done | bytes 262176 | tf_op jit(solution)/shard_map/all_to_all | solution.py:35
  56.9 1.3 fusion.17
  58.1 0.0 all-gather.3.cloned.1.call-update
  58.2 0.0 all-gather.5.cloned.1.call-start
  58.2 0.7 all-gather.5.cloned.1.call-update
  58.9 205.2 %all-gather.3.cloned.1.call-done = bf16[512,4096]{1,0:T(8,128)(2,1)} async-done(((bf16[512,128]{1,0:T(8,128)(2,1)}), bf16[512,4096]{1,0:T(8,128)(2,1)}) %all-gather.3.cloned.1.call-update) | async-done | bytes 4194320 | tf_op jit(solution)/shard_map/all_gather | solution.py:57
  264.1 6.5 %copy.14 = bf16[512,4096]{0,1:T(8,128)(2,1)} copy(bf16[512,4096]{1,0:T(8,128)(2,1)} %all-gather.3.cloned.1.call-done) | data formatting | bytes 8388608 | tf_op jit(solution)/shard_map/all_gather | solution.py:57
  270.6 4.0 fusion.47
  274.6 88.1 %all-gather.5.cloned.1.call-done = bf16[2,2048,512]{2,1,0:T(8,128)(2,1)} async-done(((bf16[2,128,512]{2,1,0:T(8,128)(2,1)}), bf16[2,2048,512]{2,1,0:T(8,128)(2,1)}) %all-gather.5.cloned.1.call-update) | async-done | bytes 4194320 | tf_op jit(solution)/shard_map/all_gather | solution.py:61
  362.7 0.0 copy-start.1
  362.7 3.0 fusion.7
  365.7 0.0 copy-done.1
  365.7 0.0 copy-start.2
  365.7 0.0 copy-start.3
  365.8 3.0 fusion.6
  368.8 0.0 copy-done.2
  368.8 0.1 copy-done.3
  368.8 1.3 fusion.11
  370.1 1.3 fusion.15
  371.5 48.4 %psum.7 = f32[512]{0:T(512)} all-reduce(f32[512]{0:T(512)S(1)} %fusion.15), channel_id=1, replica_groups=mesh['slab'=16,'src'=32] {'slab'}, use_global_device_ids=true, to_apply=%region_4.5 | all-reduce | flops 512 | bytes 4096 | tf_op jit(solution)/shard_map/psum | solution.py:74
  (6 shorter events, 0.1 us)
Async XLA Ops:
  6.5 19.5 %copy-start = (bf16[1,512,128]{2,1,0:T(8,128)(2,1)S(1)}, bf16[1,512,128]{2,1,0:T(8,128)(2,1)}, u32[]{:S(2)}) copy-start(bf16[1,512,128]{2,1,0:T(8,128)(2,1)} %param.5) | copy-start | bytes 393220
  12.0 23.8 %all-to-all-start = ((bf16[16,64,2]{1,2,0:T(2,128)(2,1)}), bf16[16,64,2]{1,2,0:T(2,128)(2,1)S(1)}, u32[]{:S(2)}, u32[]{:S(2)}) async-start(bf16[16,64,2]{1,2,0:T(2,128)(2,1)} %copy.12), calls=%async_computation | async-start | bytes 16384 | tf_op jit(solution)/shard_map/all_to_all | solution.py:42
  35.7 21.1 %all-to-all-start.1 = ((bf16[16,64,128]{2,1,0:T(8,128)(2,1)}), bf16[16,64,128]{2,1,0:T(8,128)(2,1)S(1)}, u32[]{:S(2)}, u32[]{:S(2)}) async-start(bf16[16,64,128]{2,1,0:T(8,128)(2,1)} %bitcast.6), calls=%async_computation.1 | async-start | bytes 524288 | tf_op jit(solution)/shard_map/all_to_all | solution.py:35
  39.8 224.3 %all-gather.3.cloned.1.call-start = ((), (), s32[]{:S(2)}) async-start(), calls=%async_computation.2 | async-start | bytes 4325376 | tf_op jit(solution)/shard_map/all_gather | solution.py:57
  58.2 304.6 %all-gather.5.cloned.1.call-start = ((), (), s32[]{:S(2)}) async-start(), calls=%async_computation.3 | async-start | bytes 4456448 | tf_op jit(solution)/shard_map/all_gather | solution.py:61
  362.7 3.0 copy-start.1
  365.7 3.0 copy-start.2
  365.7 3.1 copy-start.3
Sparse Core Ops, SparseCore 0:
  58.3 205.7 all-gather.2
  266.2 96.4 all-gather.4
where the time goes:
time: 432 us; the launch traced here: 427 us
  waiting for transfers between devices  319 us (74%)
  blocking collectives  48.4 us (11%)
  starting transfers between devices  18.2 us (4%)
  between operations  13.5 us (3%)
  local copies, waits for them, and re-layouts  11.6 us (3%)
  matrix products  11.5 us (3%)
    all_gather x1, waiting for transfers between devices, on_device(): residual_rows = lax.all_gather(residual_piece, 'src', axis=1, tiled=True)  205 us
    all_gather x1, waiting for transfers between devices, on_device(): piece = lax.all_gather(green_fields, 'slab', axis=1, tiled=True)  88.1 us
    psum x1, blocking collectives, on_device(): return lax.psum(partial_value, 'slab')  48.4 us
    all_to_all x1, waiting for transfers between devices, on_device(): lax.all_to_all(sent_values.reshape(slab_count, capacity, width), 'slab',...  16.9 us
    all_to_all x1, starting transfers between devices, on_device(): lax.all_to_all(sent_labels.reshape(slab_count, capacity, 2), 'slab', spli...  14 us
  transfers between devices with their start and end apart: 4, of which 4 were waited for; matrix products, arithmetic and copies ran while one was open for 3% of the time, Pallas kernels for 0%

commit v1 on v0

v1 whole, which is shorter than its diff:
```python
import jax
import jax.numpy as jnp
from jax import lax
from jax.experimental import pallas as pl
from jax.experimental.pallas import tpu as pltpu
from jax.sharding import PartitionSpec as P

MESH = pl.DeviceIdType.MESH
SLABS = 16
SRCS = 32
CAP = 64
ROWS = 512
CELLS = 512
CHIPS = 8


def kernel(
    owner_ref,
    label_ref,
    values_ref,
    fields_hbm,
    green_hbm,
    out_ref,
    sent,
    sent_labels,
    got,
    got_labels,
    res,
    green,
    fields,
    acc_re,
    acc_im,
    parts,
    load_sem,
    trace_send,
    trace_recv,
    label_send,
    label_recv,
    green_send,
    green_recv,
    pair_send,
    pair_recv,
    res_send,
    res_recv,
    sum_send,
    sum_recv,
):
    slab = lax.axis_index("slab")
    src = lax.axis_index("src")
    z, core = slab // 2, slab % 2
    y, x, h = src // 8, (src // 2) % 4, src % 2

    def at(dx, dy, hh):
        return (((y + dy + 4) % 4) * 4 + (x + dx + 4) % 4) * 2 + hh

    neighbours = (at(1, 0, h), at(-1, 0, h), at(0, 1, h), at(0, -1, h))
    twin = at(0, 0, 1 - h)

    load_green = pltpu.make_async_copy(green_hbm, green.at[slab], load_sem.at[0])
    load_green.start()
    load_fields = pltpu.make_async_copy(fields_hbm, fields, load_sem.at[1])
    load_fields.start()

    barrier = pltpu.get_barrier_semaphore()
    for d in range(1, SLABS):
        pl.semaphore_signal(
            barrier, inc=1, device_id={"slab": (slab + d) % SLABS}, device_id_type=MESH
        )
    for other in neighbours + (twin,):
        pl.semaphore_signal(barrier, inc=1, device_id={"src": other}, device_id_type=MESH)

    owners = owner_ref[...]
    labels = label_ref[...]
    owner_ids = lax.broadcasted_iota(jnp.int32, (SLABS, ROWS), 0)
    hits = owner_ids == owners
    hits_f = hits.astype(jnp.float32)
    earlier = (
        lax.broadcasted_iota(jnp.int32, (ROWS, ROWS), 0)
        < lax.broadcasted_iota(jnp.int32, (ROWS, ROWS), 1)
    )
    counts = jnp.dot(
        hits_f.astype(jnp.bfloat16),
        earlier.astype(jnp.float32).astype(jnp.bfloat16),
        preferred_element_type=jnp.float32,
    )
    ranks = jnp.sum(counts * hits_f, axis=0, keepdims=True).astype(jnp.int32)
    slots = owners * CAP + ranks
    placing = (
        (lax.broadcasted_iota(jnp.int32, (SLABS * CAP, ROWS), 0) == slots)
        .astype(jnp.float32)
        .astype(jnp.bfloat16)
    )
    placed = jnp.dot(placing, values_ref[...], preferred_element_type=jnp.float32)
    sent[...] = placed.astype(jnp.bfloat16).reshape(SLABS, CAP, 128)
    rank_hits = (
        (lax.broadcasted_iota(jnp.int32, (128, ROWS), 0) % CAP == ranks)
        .astype(jnp.float32)
        .astype(jnp.bfloat16)
    )
    high = (labels // 32).astype(jnp.float32)
    low = (labels % 32 + 1).astype(jnp.float32)
    codes = jnp.concatenate([hits_f * high, hits_f * low], axis=0).astype(jnp.bfloat16)
    placed_codes = lax.dot_general(
        codes, rank_hits, (((1,), (1,)), ((), ())), preferred_element_type=jnp.float32
    )
    label_rows = placed_codes[:SLABS] * 32.0 + placed_codes[SLABS:] - 1.0
    for k in range(SLABS):
        sent_labels[k] = label_rows[k : k + 1, :]

    load_green.wait()
    pl.semaphore_wait(barrier, SLABS - 1 + 5)

    def trace_copy(d):
        to = (slab + d) % SLABS
        return (
            pltpu.make_async_remote_copy(
                src_ref=sent.at[to],
                dst_ref=got.at[slab],
                send_sem=trace_send.at[d],
                recv_sem=trace_recv.at[slab],
                device_id={"slab": to},
                device_id_type=MESH,
            ),
            pltpu.make_async_remote_copy(
                src_ref=sent_labels.at[to],
                dst_ref=got_labels.at[slab],
                send_sem=label_send.at[d],
                recv_sem=label_recv.at[slab],
                device_id={"slab": to},
                device_id_type=MESH,
            ),
        )

    def trace_wait(d):
        frm = (slab + d) % SLABS
        pltpu.make_async_copy(got.at[frm], got.at[frm], trace_recv.at[frm]).wait()
        pltpu.make_async_copy(got_labels.at[frm], got_labels.at[frm], label_recv.at[frm]).wait()

    for d in range(1, SLABS):
        for copy in trace_copy(d):
            copy.start()

    def green_copy(step, block, part, way):
        index = block * 2 + core
        to = (slab + 2, slab - 2)[way]
        return pltpu.make_async_remote_copy(
            src_ref=green.at[index, part],
            dst_ref=green.at[index, part],
            send_sem=green_send.at[way, step, part],
            recv_sem=green_recv.at[index, part],
            device_id={"slab": to},
            device_id_type=MESH,
        )

    def pair_copy(block, part):
        index = block * 2 + core
        return pltpu.make_async_remote_copy(
            src_ref=green.at[index, part],
            dst_ref=green.at[index, part],
            send_sem=pair_send.at[block, part],
            recv_sem=pair_recv.at[block, part],
            device_id={"slab": z * 2 + 1 - core},
            device_id_type=MESH,
        )

    def green_wait(block, part):
        index = block * 2 + core
        pltpu.make_async_copy(
            green.at[index, part], green.at[index, part], green_recv.at[index, part]
        ).wait()

    def green_step(step):
        for part in range(2):
            if step == 0:

                @pl.when(z < CHIPS - 1)
                def _():
                    green_copy(0, z, part, 0).start()

                @pl.when(z > 0)
                def _():
                    green_copy(0, z, part, 1).start()

                pair_copy(z, part).start()
            else:

                @pl.when(z >= step)
                def _():
                    green_wait(z - step, part)

                    @pl.when(z < CHIPS - 1)
                    def _():
                        green_copy(step, z - step, part, 0).start()

                    pair_copy(z - step, part).start()

                @pl.when(z + step < CHIPS)
                def _():
                    green_wait(z + step, part)

                    @pl.when(z > 0)
                    def _():
                        green_copy(step, z + step, part, 1).start()

                    pair_copy(z + step, part).start()

    def block_of(half, a, b, hh):
        return at(a, b, hh) if half == 0 else at(b, a, hh)

    def res_copy(half, a, b, hh, quarter, way):
        first = half * 256 + max(quarter, 0) * 128
        count = 256 if quarter < 0 else 128
        block = block_of(half, a, b, hh)
        da, db = way
        to = block_of(half, da, db, h)
        ref = res.at[block, pl.ds(first, count), :]
        return pltpu.make_async_remote_copy(
            src_ref=ref,
            dst_ref=ref,
            send_sem=res_send,
            recv_sem=res_recv.at[block, half * 2 + max(quarter, 0)],
            device_id={"src": to},
            device_id_type=MESH,
        )

    def res_wait(half, a, b, hh, quarter):
        first = half * 256 + max(quarter, 0) * 128
        count = 256 if quarter < 0 else 128
        block = block_of(half, a, b, hh)
        ref = res.at[block, pl.ds(first, count), :]
        pltpu.make_async_copy(ref, ref, res_recv.at[block, half * 2 + max(quarter, 0)]).wait()

    RIGHT, LEFT, UP, DOWN = (1, 0), (-1, 0), (0, 1), (0, -1)

    def res_round(step, hh):
        for half in range(2):
            if step == 0:
                res_copy(half, 0, 0, hh, -1, RIGHT).start()
                res_copy(half, 0, 0, hh, -1, LEFT).start()
            elif step == 1:
                res_wait(half, -1, 0, hh, -1)
                res_copy(half, -1, 0, hh, 0, RIGHT).start()
                res_wait(half, 1, 0, hh, -1)
                res_copy(half, 1, 0, hh, 1, LEFT).start()
            elif step == 2:
                res_wait(half, 2, 0, hh, 0)
                res_wait(half, 2, 0, hh, 1)
            elif step == 3:
                for a in (0, -1, 1):
                    res_wait(half, a, -1, hh, -1)
                    res_copy(half, a, -1, hh, 0, UP).start()
                    res_wait(half, a, 1, hh, -1)
                    res_copy(half, a, 1, hh, 1, DOWN).start()
            elif step == 4:
                res_wait(half, 2, -1, hh, -1)
                res_copy(half, 2, -1, hh, 0, UP).start()
                res_wait(half, 2, 1, hh, -1)
                res_copy(half, 2, 1, hh, 1, DOWN).start()
            else:
                for a in (0, -1, 1, 2):
                    res_wait(half, a, 2, hh, 0)
                    res_wait(half, a, 2, hh, 1)
        if step < 3:
            for half in range(2):
                for a in ((0,), (-1, 1), (2,))[step]:
                    res_copy(half, a, 0, hh, -1, UP).start()
                    res_copy(half, a, 0, hh, -1, DOWN).start()

    green_step(0)
    green_step(1)
    got[slab] = sent[slab]
    got_labels[slab] = sent_labels[slab]
    for d in range(1, SLABS):
        trace_wait(d)
    low_lanes = lax.broadcasted_iota(jnp.int32, (1, 128), 1) < CAP
    rows_f = lax.broadcasted_iota(jnp.int32, (ROWS, 128), 0).astype(jnp.float32)
    picks = []
    for i in range(SLABS // 2):
        row = jnp.where(low_lanes, got_labels[2 * i], got_labels[2 * i + 1])
        picks.append((rows_f == row).astype(jnp.float32).astype(jnp.bfloat16))
    assembled = jnp.dot(
        jnp.concatenate(picks, axis=1),
        got[...].reshape(SLABS * CAP, 128),
        preferred_element_type=jnp.float32,
    )
    res[src] = assembled.astype(jnp.bfloat16)

    twin_copy = pltpu.make_async_remote_copy(
        src_ref=res.at[src],
        dst_ref=res.at[src],
        send_sem=trace_send.at[0],
        recv_sem=trace_recv.at[SLABS],
        device_id={"src": twin},
        device_id_type=MESH,
    )
    twin_copy.start()
    res_round(0, h)
    green_step(2)
    res_round(1, h)
    res_round(2, h)
    green_step(3)
    res_round(3, h)
    pltpu.make_async_copy(res.at[twin], res.at[twin], trace_recv.at[SLABS]).wait()
    res_round(0, 1 - h)
    res_round(4, h)
    green_step(4)
    res_round(1, 1 - h)
    res_round(5, h)
    res_round(2, 1 - h)
    green_step(5)
    res_round(3, 1 - h)
    green_step(6)
    res_round(4, 1 - h)
    green_step(7)
    res_round(5, 1 - h)

    acc_re[...] = jnp.zeros_like(acc_re)
    acc_im[...] = jnp.zeros_like(acc_im)
    load_fields.wait()

    def multiply(block, carry):
        for part in range(2):
            other = block * 2 + 1 - core
            pltpu.make_async_copy(
                green.at[other, part], green.at[other, part], pair_recv.at[block, part]
            ).wait()
        for i in range(2):
            index = block * 2 + i
            left = jnp.concatenate([res[2 * index], res[2 * index + 1]], axis=1)
            g_re = green[index, 0]
            g_im = green[index, 1]
            half = CAP
            right_re = jnp.concatenate([g_re[:half], g_im[:half], g_re[half:], g_im[half:]], axis=0)
            right_im = jnp.concatenate(
                [g_im[:half], -g_re[:half], g_im[half:], -g_re[half:]], axis=0
            )
            acc_re[...] += jnp.dot(left, right_re, preferred_element_type=jnp.float32)
            acc_im[...] += jnp.dot(left, right_im, preferred_element_type=jnp.float32)
        return carry

    lax.fori_loop(0, CHIPS, multiply, 0)
    partial = jnp.sum(
        fields[0].astype(jnp.float32) * acc_re[...] - fields[1].astype(jnp.float32) * acc_im[...],
        axis=0,
        keepdims=True,
    )
    parts[slab] = partial

    def sum_copy(d):
        return pltpu.make_async_remote_copy(
            src_ref=parts.at[slab],
            dst_ref=parts.at[slab],
            send_sem=sum_send.at[d],
            recv_sem=sum_recv.at[slab],
            device_id={"slab": (slab + d) % SLABS},
            device_id_type=MESH,
        )

    for d in range(1, SLABS):
        sum_copy(d).start()

    for d in range(1, SLABS):
        for copy in trace_copy(d):
            copy.wait_send()
    twin_copy.wait_send()
    for part in range(2):
        for step in range(CHIPS):

            @pl.when((z >= step) & (z < CHIPS - 1))
            def _():
                green_copy(step, z, part, 0).wait_send()

            @pl.when((z + step < CHIPS) & (z > 0))
            def _():
                green_copy(step, z, part, 1).wait_send()

            pair_copy(step, part).wait_send()
    pltpu.make_async_copy(res.at[pl.ds(0, 30)], res.at[pl.ds(0, 30)], res_send).wait()

    for d in range(1, SLABS):
        frm = (slab + d) % SLABS
        pltpu.make_async_copy(parts.at[frm], parts.at[frm], sum_recv.at[frm]).wait()
    out_ref[...] = jnp.sum(parts[...], axis=0)
    for d in range(1, SLABS):
        sum_copy(d).wait_send()


def on_device(trace_values, trace_owner, trace_source, source_fields, green_fields):
    dma = pltpu.SemaphoreType.DMA
    vmem = pl.BlockSpec(memory_space=pltpu.VMEM)
    anyspace = pl.BlockSpec(memory_space=pltpu.HBM)
    out = pl.pallas_call(
        kernel,
        out_shape=jax.ShapeDtypeStruct((1, CELLS), jnp.float32),
        in_specs=[vmem, vmem, vmem, anyspace, anyspace],
        out_specs=vmem,
        scratch_shapes=[
            pltpu.VMEM((SLABS, CAP, 128), jnp.bfloat16),
            pltpu.VMEM((SLABS, 1, 128), jnp.float32),
            pltpu.VMEM((SLABS, CAP, 128), jnp.bfloat16),
            pltpu.VMEM((SLABS, 1, 128), jnp.float32),
            pltpu.VMEM((SRCS, ROWS, 128), jnp.bfloat16),
            pltpu.VMEM((SLABS, 2, 128, CELLS), jnp.bfloat16),
            pltpu.VMEM((2, ROWS, CELLS), jnp.bfloat16),
            pltpu.VMEM((ROWS, CELLS), jnp.float32),
            pltpu.VMEM((ROWS, CELLS), jnp.float32),
            pltpu.VMEM((SLABS, 1, CELLS), jnp.float32),
            dma((2,)),
            dma((SLABS,)),
            dma((SLABS + 1,)),
            dma((SLABS,)),
            dma((SLABS,)),
            dma((2, CHIPS, 2)),
            dma((SLABS, 2)),
            dma((CHIPS, 2)),
            dma((CHIPS, 2)),
            dma,
            dma((SRCS, 4)),
            dma((SLABS,)),
            dma((SLABS,)),
        ],
        compiler_params=pltpu.CompilerParams(
            collective_id=0, has_side_effects=True, vmem_limit_bytes=60 * 1024 * 1024
        ),
    )(
        trace_owner.reshape(1, ROWS),
        trace_source.reshape(1, ROWS),
        trace_values[0],
        source_fields,
        green_fields,
    )
    return out.reshape(CELLS)


def solution(mesh):
    in_specs = (
        P("src", "slab", None),
        P("src", "slab", None),
        P("src", "slab"),
        P(None, "slab", "src"),
        P(None, "slab", "src"),
    )
    return jax.shard_map(
        on_device, mesh=mesh, in_specs=in_specs, out_specs=P("src"), check_vma=False
    )
```

time: 432 us -> 97.7 us (0.23); the launches traced: 427 us -> 97.6 us
  waiting for transfers between devices: 319 us -> 0 us
  Pallas kernels: 0 us -> 96.3 us
  blocking collectives: 48.4 us -> 0 us
  starting transfers between devices: 18.2 us -> 0 us
  between operations: 13.5 us -> 0.01 us
  matrix products: 11.5 us -> 0 us
  local copies, waits for them, and re-layouts: 11.6 us -> 1.26 us
    all_gather x2 -> x0, waiting for transfers between devices: 293 us -> none  [the longest x1 205 us: on_device(): residual_rows = lax.all_gather(residual_piece, 'src', axis=1, tiled=True)]
    pallas_call x0 -> x1, Pallas kernels: none -> 96.3 us  [on_device(): pl.pallas_call(kernel, out_shape=jax.ShapeDtypeStruct((1, CELLS), jnp.flo...]
    psum x1 -> x0, blocking collectives: 48.4 us -> none  [on_device(): return lax.psum(partial_value, 'slab')]
    all_to_all x2 -> x0, waiting for transfers between devices: 25.4 us -> none  [the longest x1 16.9 us: on_device(): lax.all_to_all(sent_values.reshape(slab_count, capacity, width), 'slab',...]
    all_to_all x2 -> x0, starting transfers between devices: 18.1 us -> none  [the longest x1 14 us: on_device(): lax.all_to_all(sent_labels.reshape(slab_count, capacity, 2), 'slab', spli...]
    dot_general x7 -> x0, matrix products: 11.5 us -> none  [the longest x1 3.02 us: on_device(): jnp.dot(res_imag, piece[0], preferred_element_type=jnp.float32)]
    all_gather x1 -> x0, local copies, waits for them, and re-layouts: 6.52 us -> none  [on_device(): residual_rows = lax.all_gather(residual_piece, 'src', axis=1, tiled=True)]
  transfers between devices with their start and end apart: 4 -> 0, of which waited for: 4 -> 0; matrix products, arithmetic and copies ran while one was open for 3% -> 0% of each run, Pallas kernels for 0% -> 0%
where the time goes in v1:
time: 97.7 us; the launch traced here: 97.6 us
  Pallas kernels  96.3 us (99%)
  local copies, waits for them, and re-layouts  1.26 us (1%)
    pallas_call x1, Pallas kernels, on_device(): pl.pallas_call(kernel, out_shape=jax.ShapeDtypeStruct((1, CELLS), jnp.flo...  96.3 us

profile of v1, /device:TPU:1, one launch (start us, length us, event | category | flops | bytes accessed | tf_op | source)
XLA Modules:
  0.0 97.6 jit_solution(1800062331127662108)
XLA Ops:
  0.0 96.3 %shard_map.55 = f32[1,512]{1,0:T(1,128)} custom-call(s32[1,512]{1,0:T(1,128)} %bitcast.5, s32[1,512]{1,0:T(1,128)} %label_ref.1, bf16[512,128]{1,0:T(8,128)(2,1)} %bitcast.3, bf16[2,512,512]{2,1,0:T(8,128)(2,1)} %fields_hbm.1, bf16[2,128,512]{2,1,0:T(8,128)(2,1)} %green_hbm.1), custom_call_target="tpu_custom_call" | custom-call | tf_op jit(solution)/shard_map/pallas_call | solution.py:392
  96.3 1.3 %copy.7 = f32[512]{0:T(512)} copy(f32[512]{0:T(512)} %bitcast.4) | data formatting | bytes 4096

commit v2 on v1

v2 whole, which is shorter than its diff:
```python
import jax
import jax.numpy as jnp
from jax import lax
from jax.experimental import pallas as pl
from jax.experimental.pallas import tpu as pltpu
from jax.sharding import PartitionSpec as P

MESH = pl.DeviceIdType.MESH
SLABS = 16
SRCS = 32
CAP = 64
ROWS = 512
CELLS = 512
CHIPS = 8
RING = 16
EARLY_STEPS = 5


def kernel(
    owner_hbm,
    label_hbm,
    values_hbm,
    fields_hbm,
    green_hbm,
    out_ref,
    owner_ref,
    label_ref,
    values_ref,
    sent,
    sent_labels,
    got,
    got_labels,
    res,
    green,
    fields,
    acc_re,
    acc_im,
    parts,
    load_sem,
    trace_sem,
    green_send,
    green_recv,
    pair_send,
    pair_recv,
    twin_sem,
    res_send,
    res_recv,
    sum_sem,
    from_left,
    from_right,
):
    slab = lax.axis_index("slab")
    src = lax.axis_index("src")
    z, core = slab // 2, slab % 2
    y, x, h = src // 8, (src // 2) % 4, src % 2
    ring = h * CHIPS + z

    loads = []
    for i, (a, b) in enumerate(
        (
            (owner_hbm, owner_ref),
            (label_hbm, label_ref),
            (values_hbm, values_ref),
            (green_hbm, green.at[slab]),
            (fields_hbm, fields),
        )
    ):
        loads.append(pltpu.make_async_copy(a, b, load_sem.at[i]))
        loads[-1].start()

    def at(dx, dy, hh):
        return (((y + dy + 4) % 4) * 4 + (x + dx + 4) % 4) * 2 + hh

    def along(d, to_core=core):
        to = (ring + d + RING) % RING
        return {"slab": (to % CHIPS) * 2 + to_core, "src": src - h + to // CHIPS}

    barrier = pltpu.get_barrier_semaphore()
    neighbours = [along(1), along(-1), {"slab": z * 2 + 1 - core}]
    neighbours += [along(1, 1 - core), along(-1, 1 - core)]
    neighbours += [{"src": at(1, 0, h)}, {"src": at(-1, 0, h)}]
    neighbours += [{"src": at(0, 1, h)}, {"src": at(0, -1, h)}]
    for other in neighbours:
        pl.semaphore_signal(barrier, inc=1, device_id=other, device_id_type=MESH)

    loads[0].wait()
    loads[1].wait()
    owners = owner_ref[...]
    labels = label_ref[...]
    hits = lax.broadcasted_iota(jnp.int32, (SLABS, ROWS), 0) == owners
    hits_f = hits.astype(jnp.float32)
    earlier = lax.broadcasted_iota(jnp.int32, (ROWS, ROWS), 0) < lax.broadcasted_iota(
        jnp.int32, (ROWS, ROWS), 1
    )
    counts = jnp.dot(
        hits_f.astype(jnp.bfloat16),
        earlier.astype(jnp.float32).astype(jnp.bfloat16),
        preferred_element_type=jnp.float32,
    )
    ranks = jnp.sum(counts * hits_f, axis=0, keepdims=True).astype(jnp.int32)
    slots = owners * CAP + ranks
    placing = (
        (lax.broadcasted_iota(jnp.int32, (SLABS * CAP, ROWS), 0) == slots)
        .astype(jnp.float32)
        .astype(jnp.bfloat16)
    )
    rank_hits = (
        (lax.broadcasted_iota(jnp.int32, (128, ROWS), 0) % CAP == ranks)
        .astype(jnp.float32)
        .astype(jnp.bfloat16)
    )
    high = (labels // 32).astype(jnp.float32)
    low = (labels % 32 + 1).astype(jnp.float32)
    codes = jnp.concatenate([hits_f * high, hits_f * low], axis=0).astype(jnp.bfloat16)
    placed_codes = lax.dot_general(
        codes, rank_hits, (((1,), (1,)), ((), ())), preferred_element_type=jnp.float32
    )
    label_rows = placed_codes[:SLABS] * 32.0 + placed_codes[SLABS:] - 1.0
    for k in range(SLABS):
        sent_labels[k] = label_rows[k : k + 1, :]
    loads[2].wait()
    placed = jnp.dot(placing, values_ref[...], preferred_element_type=jnp.float32)
    sent[...] = placed.astype(jnp.bfloat16).reshape(SLABS, CAP, 128)

    def green_copy(block, part, d):
        ref = green.at[block * 2 + core, part]
        return pltpu.make_async_remote_copy(
            src_ref=ref,
            dst_ref=ref,
            send_sem=green_send,
            recv_sem=green_recv.at[block, part],
            device_id={"slab": slab + 2 * d},
            device_id_type=MESH,
        )

    def pair_copy(block, part):
        ref = green.at[block * 2 + core, part]
        return pltpu.make_async_remote_copy(
            src_ref=ref,
            dst_ref=ref,
            send_sem=pair_send,
            recv_sem=pair_recv.at[block],
            device_id={"slab": z * 2 + 1 - core},
            device_id_type=MESH,
        )

    def green_wait(block, part):
        ref = green.at[block * 2 + core, part]
        pltpu.make_async_copy(ref, ref, green_recv.at[block, part]).wait()

    def green_start():
        for part in range(2):

            @pl.when(z < CHIPS - 1)
            def _():
                green_copy(z, part, 1).start()

            @pl.when(z > 0)
            def _():
                green_copy(z, part, -1).start()

        for part in range(2):
            pair_copy(z, part).start()

    def green_step(step):
        for part in range(2):

            @pl.when(z >= step)
            def _():
                green_wait(z - step, part)

                @pl.when(z < CHIPS - 1)
                def _():
                    green_copy(z - step, part, 1).start()

                pair_copy(z - step, part).start()

            @pl.when(z + step < CHIPS)
            def _():
                green_wait(z + step, part)

                @pl.when(z > 0)
                def _():
                    green_copy(z + step, part, -1).start()

                pair_copy(z + step, part).start()

    def trace_send(to):
        pltpu.make_async_remote_copy(
            src_ref=sent.at[to],
            dst_ref=got.at[slab],
            send_sem=trace_sem.at[0],
            recv_sem=trace_sem.at[1],
            device_id={"slab": to},
            device_id_type=MESH,
        ).start()
        pltpu.make_async_remote_copy(
            src_ref=sent_labels.at[to],
            dst_ref=got_labels.at[slab],
            send_sem=trace_sem.at[2],
            recv_sem=trace_sem.at[3],
            device_id={"slab": to},
            device_id_type=MESH,
        ).start()

    def all_traces(i):
        ref = (got, got_labels)[i // 2].at[pl.ds(0, SLABS - 1)]
        pltpu.make_async_copy(ref, ref, trace_sem.at[i]).wait()

    def trace_steps():
        for s in range(1, CHIPS + 1):
            if s > 1:
                pl.semaphore_wait(from_left.at[s - 2], 1)
            if s < CHIPS:
                pl.semaphore_signal(
                    from_left.at[s - 1], inc=1, device_id=along(1), device_id_type=MESH
                )

                @pl.when(z >= s)
                def _():
                    for other in range(2):
                        trace_send((z - s) * 2 + other)

                @pl.when(z + s < CHIPS)
                def _():
                    if s > 1:
                        pl.semaphore_wait(from_right.at[s - 2], 1)

                    @pl.when(z > 0)
                    def _():
                        pl.semaphore_signal(
                            from_right.at[s - 1], inc=1, device_id=along(-1), device_id_type=MESH
                        )

                    for other in range(2):
                        trace_send((z + s) * 2 + other)

    def block_of(half, a, b, hh):
        return at(a, b, hh) if half == 0 else at(b, a, hh)

    def res_copy(half, a, b, hh, quarter, way, sem):
        first = half * 256 + max(quarter, 0) * 128
        ref = res.at[block_of(half, a, b, hh), pl.ds(first, 256 if quarter < 0 else 128), :]
        pltpu.make_async_remote_copy(
            src_ref=ref,
            dst_ref=ref,
            send_sem=res_send,
            recv_sem=res_recv.at[sem],
            device_id={"src": block_of(half, way[0], way[1], h)},
            device_id_type=MESH,
        ).start()

    RIGHT, LEFT, UP, DOWN = (1, 0), (-1, 0), (0, 1), (0, -1)

    def res_round(step, turn):
        hh = (h, 1 - h)[turn]
        for half in range(2):

            def sem(number):
                return (turn * 5 + number - 1) * 2 + half

            if step > 0:
                ref = (
                    res.at[0],
                    res.at[0, pl.ds(0, 256), :],
                    res.at[pl.ds(0, 3)],
                    res.at[0],
                    res.at[pl.ds(0, 2)],
                )[step - 1]
                pltpu.make_async_copy(ref, ref, res_recv.at[sem(step)]).wait()
            if step == 0:
                res_copy(half, 0, 0, hh, -1, RIGHT, sem(1))
                res_copy(half, 0, 0, hh, -1, LEFT, sem(1))
            elif step == 1:
                res_copy(half, -1, 0, hh, 0, RIGHT, sem(2))
                res_copy(half, 1, 0, hh, 1, LEFT, sem(2))
            elif step == 3:
                for a in (0, -1, 1):
                    res_copy(half, a, -1, hh, 0, UP, sem(5))
                    res_copy(half, a, 1, hh, 1, DOWN, sem(5))
            elif step == 4:
                res_copy(half, 2, -1, hh, 0, UP, sem(5))
                res_copy(half, 2, 1, hh, 1, DOWN, sem(5))
        if step < 3:
            for half in range(2):
                number = (turn * 5 + (3 if step < 2 else 4) - 1) * 2 + half
                for a in ((0,), (-1, 1), (2,))[step]:
                    res_copy(half, a, 0, hh, -1, UP, number)
                    res_copy(half, a, 0, hh, -1, DOWN, number)

    loads[3].wait()
    pl.semaphore_wait(barrier, len(neighbours))
    late = (ring >= 6) & (ring < 10)

    @pl.when(jnp.logical_not(late))
    def _():
        green_start()

    trace_send(z * 2 + 1 - core)
    trace_steps()

    @pl.when(late)
    def _():
        green_start()

    got[slab] = sent[slab]
    got_labels[slab] = sent_labels[slab]
    green_step(1)
    all_traces(1)
    all_traces(3)
    low_lanes = lax.broadcasted_iota(jnp.int32, (1, 128), 1) < CAP
    rows_f = lax.broadcasted_iota(jnp.int32, (ROWS, 128), 0).astype(jnp.float32)
    picks = []
    for i in range(SLABS // 2):
        row = jnp.where(low_lanes, got_labels[2 * i], got_labels[2 * i + 1])
        picks.append((rows_f == row).astype(jnp.float32).astype(jnp.bfloat16))
    assembled = jnp.dot(
        jnp.concatenate(picks, axis=1),
        got[...].reshape(SLABS * CAP, 128),
        preferred_element_type=jnp.float32,
    )
    res[src] = assembled.astype(jnp.bfloat16)

    twin = at(0, 0, 1 - h)
    twin_copy = pltpu.make_async_remote_copy(
        src_ref=res.at[src],
        dst_ref=res.at[src],
        send_sem=twin_sem.at[0],
        recv_sem=twin_sem.at[1],
        device_id={"src": twin},
        device_id_type=MESH,
    )
    twin_copy.start()
    res_round(0, 0)
    green_step(2)
    res_round(1, 0)
    res_round(2, 0)
    green_step(3)
    res_round(3, 0)
    res_round(4, 0)
    pltpu.make_async_copy(res.at[twin], res.at[twin], twin_sem.at[1]).wait()
    res_round(0, 1)
    res_round(5, 0)
    green_step(4)
    res_round(1, 1)
    res_round(2, 1)
    green_step(5)
    acc_re[...] = jnp.zeros_like(acc_re)
    acc_im[...] = jnp.zeros_like(acc_im)
    loads[4].wait()
    res_round(3, 1)
    res_round(4, 1)
    res_round(5, 1)

    def chip_of(n):
        m = jnp.minimum(z, CHIPS - 1 - z)
        side = z + jnp.where(n % 2 == 1, -((n + 1) // 2), n // 2)
        rest = jnp.where(z < CHIPS // 2, n, CHIPS - 1 - n)
        return jnp.where(n <= 2 * m, side, rest)

    def multiply(n, carry):
        block = chip_of(n)
        far = jnp.abs(block - z)
        before = jnp.abs(chip_of(jnp.maximum(n - 1, 0)) - z)

        @pl.when((far > EARLY_STEPS) & (far > before))
        def _():
            green_step(far)

        ref = green.at[block * 2 + 1 - core]
        pltpu.make_async_copy(ref, ref, pair_recv.at[block]).wait()
        for i in range(2):
            index = block * 2 + i
            left = jnp.concatenate([res[2 * index], res[2 * index + 1]], axis=1)
            g_re = green[index, 0]
            g_im = green[index, 1]
            right_re = jnp.concatenate([g_re[:CAP], g_im[:CAP], g_re[CAP:], g_im[CAP:]], axis=0)
            right_im = jnp.concatenate([g_im[:CAP], -g_re[:CAP], g_im[CAP:], -g_re[CAP:]], axis=0)
            acc_re[...] += jnp.dot(left, right_re, preferred_element_type=jnp.float32)
            acc_im[...] += jnp.dot(left, right_im, preferred_element_type=jnp.float32)
        return carry

    lax.fori_loop(0, CHIPS, multiply, 0)
    partial = jnp.sum(
        fields[0].astype(jnp.float32) * acc_re[...] - fields[1].astype(jnp.float32) * acc_im[...],
        axis=0,
        keepdims=True,
    )
    parts[slab] = partial
    for d in range(1, SLABS):
        pltpu.make_async_remote_copy(
            src_ref=parts.at[slab],
            dst_ref=parts.at[slab],
            send_sem=sum_sem.at[0],
            recv_sem=sum_sem.at[1],
            device_id={"slab": (slab + d) % SLABS},
            device_id_type=MESH,
        ).start()

    all_traces(0)
    all_traces(2)
    twin_copy.wait_send()
    end = (z == 0) | (z == CHIPS - 1)

    @pl.when(end)
    def _():
        pltpu.make_async_copy(green.at[0], green.at[0], green_send).wait()

    @pl.when(jnp.logical_not(end))
    def _():
        ref = green.at[pl.ds(0, CHIPS + 1)]
        pltpu.make_async_copy(ref, ref, green_send).wait()

    ref = green.at[pl.ds(0, CHIPS)]
    pltpu.make_async_copy(ref, ref, pair_send).wait()
    ref = res.at[pl.ds(0, SRCS - 2)]
    pltpu.make_async_copy(ref, ref, res_send).wait()

    ref = parts.at[pl.ds(0, SLABS - 1)]
    pltpu.make_async_copy(ref, ref, sum_sem.at[1]).wait()
    out_ref[...] = jnp.sum(parts[...], axis=0)
    pltpu.make_async_copy(ref, ref, sum_sem.at[0]).wait()


def on_device(trace_values, trace_owner, trace_source, source_fields, green_fields):
    dma = pltpu.SemaphoreType.DMA
    out = pl.pallas_call(
        kernel,
        out_shape=jax.ShapeDtypeStruct((1, CELLS), jnp.float32),
        in_specs=[pl.BlockSpec(memory_space=pltpu.HBM)] * 5,
        out_specs=pl.BlockSpec(memory_space=pltpu.VMEM),
        scratch_shapes=[
            pltpu.VMEM((1, ROWS), jnp.int32),
            pltpu.VMEM((1, ROWS), jnp.int32),
            pltpu.VMEM((ROWS, 128), jnp.bfloat16),
            pltpu.VMEM((SLABS, CAP, 128), jnp.bfloat16),
            pltpu.VMEM((SLABS, 1, 128), jnp.float32),
            pltpu.VMEM((SLABS, CAP, 128), jnp.bfloat16),
            pltpu.VMEM((SLABS, 1, 128), jnp.float32),
            pltpu.VMEM((SRCS, ROWS, 128), jnp.bfloat16),
            pltpu.VMEM((SLABS, 2, 128, CELLS), jnp.bfloat16),
            pltpu.VMEM((2, ROWS, CELLS), jnp.bfloat16),
            pltpu.VMEM((ROWS, CELLS), jnp.float32),
            pltpu.VMEM((ROWS, CELLS), jnp.float32),
            pltpu.VMEM((SLABS, 1, CELLS), jnp.float32),
            dma((5,)),
            dma((4,)),
            dma,
            dma((CHIPS, 2)),
            dma,
            dma((CHIPS,)),
            dma((2,)),
            dma,
            dma((20,)),
            dma((2,)),
            pltpu.SemaphoreType.REGULAR((CHIPS - 1,)),
            pltpu.SemaphoreType.REGULAR((CHIPS - 1,)),
        ],
        compiler_params=pltpu.CompilerParams(
            collective_id=0, has_side_effects=True, vmem_limit_bytes=60 * 1024 * 1024
        ),
    )(
        trace_owner.reshape(1, ROWS),
        trace_source.reshape(1, ROWS),
        trace_values[0],
        source_fields,
        green_fields,
    )
    return out.reshape(CELLS)


def solution(mesh):
    in_specs = (
        P("src", "slab", None),
        P("src", "slab", None),
        P("src", "slab"),
        P(None, "slab", "src"),
        P(None, "slab", "src"),
    )
    return jax.shard_map(
        on_device, mesh=mesh, in_specs=in_specs, out_specs=P("src"), check_vma=False
    )
```

time: 97.7 us -> 89.6 us (0.917)
  Pallas kernels: 96.3 us -> 88.2 us
    pallas_call x1, Pallas kernels: 96.3 us -> 88.2 us  [on_device(): pl.pallas_call(kernel, out_shape=jax.ShapeDtypeStruct((1, CELLS), jnp.flo...]
where the time goes in v2:
time: 89.6 us; the launch traced here: 89.5 us
  Pallas kernels  88.2 us (98%)
  local copies, waits for them, and re-layouts  1.26 us (1%)
    pallas_call x1, Pallas kernels, on_device(): pl.pallas_call(kernel, out_shape=jax.ShapeDtypeStruct((1, CELLS), jnp.flo...  88.2 us

profile of v2, /device:TPU:1, one launch (start us, length us, event | category | flops | bytes accessed | tf_op | source)
XLA Modules:
  0.0 89.5 jit_solution(14823151199765484699)
XLA Ops:
  0.0 88.2 %shard_map.55 = f32[1,512]{1,0:T(1,128)} custom-call(s32[1,512]{1,0:T(1,128)} %bitcast.5, s32[1,512]{1,0:T(1,128)} %label_hbm.1, bf16[512,128]{1,0:T(8,128)(2,1)} %bitcast.3, bf16[2,512,512]{2,1,0:T(8,128)(2,1)} %fields_hbm.1, bf16[2,128,512]{2,1,0:T(8,128)(2,1)} %green_hbm.1), custom_call_target="tpu_custom_call" | custom-call | tf_op jit(solution)/shard_map/pallas_call | solution.py:427
  88.2 1.3 %copy.7 = f32[512]{0:T(512)} copy(f32[512]{0:T(512)} %bitcast.4) | data formatting | bytes 4096

commit v3 on v2

v3 whole, which is shorter than its diff:
```python
import jax
import jax.numpy as jnp
from jax import lax
from jax.experimental import pallas as pl
from jax.experimental.pallas import tpu as pltpu
from jax.sharding import PartitionSpec as P

MESH = pl.DeviceIdType.MESH
SLABS = 16
SRCS = 32
CAP = 64
ROWS = 512
CELLS = 512
CHIPS = 8
RING = 16
EARLY_STEPS = 6


def kernel(
    owner_hbm,
    label_hbm,
    values_hbm,
    fields_hbm,
    green_hbm,
    out_ref,
    owner_ref,
    label_ref,
    values_ref,
    sent,
    sent_labels,
    got,
    got_labels,
    res,
    green,
    fields,
    acc_re,
    acc_im,
    parts,
    load_sem,
    hand_sem,
    trace_sem,
    green_send,
    green_recv,
    pair_send,
    pair_recv,
    own_sem,
    twin_sem,
    res_send,
    res_recv,
    give_send,
    give_recv,
    sum_sem,
    from_left,
    from_right,
    across,
):
    slab = lax.axis_index("slab")
    src = lax.axis_index("src")
    z, core = slab // 2, slab % 2
    y, x, h = src // 8, (src // 2) % 4, src % 2
    ring = h * CHIPS + z

    loads = []
    for i, (a, b) in enumerate(
        (
            (owner_hbm, owner_ref),
            (label_hbm, label_ref),
            (values_hbm, values_ref),
            (green_hbm, green.at[slab]),
            (fields_hbm, fields),
        )
    ):
        loads.append(pltpu.make_async_copy(a, b, load_sem.at[i]))
        loads[-1].start()

    def at(dx, dy, hh):
        return (((y + dy + 4) % 4) * 4 + (x + dx + 4) % 4) * 2 + hh

    def along(d, to_core=core):
        to = (ring + d + RING) % RING
        return {"slab": (to % CHIPS) * 2 + to_core, "src": src - h + to // CHIPS}

    barrier = pltpu.get_barrier_semaphore()
    neighbours = [along(1), along(-1), {"slab": z * 2 + 1 - core}]
    neighbours += [along(1, 1 - core), along(-1, 1 - core)]
    neighbours += [{"src": at(1, 0, h)}, {"src": at(-1, 0, h)}]
    neighbours += [{"src": at(0, 1, h)}, {"src": at(0, -1, h)}]
    for other in neighbours:
        pl.semaphore_signal(barrier, inc=1, device_id=other, device_id_type=MESH)

    loads[0].wait()
    loads[1].wait()
    owners = owner_ref[...]
    labels = label_ref[...]
    hits = lax.broadcasted_iota(jnp.int32, (SLABS, ROWS), 0) == owners
    hits_f = hits.astype(jnp.float32)
    earlier = lax.broadcasted_iota(jnp.int32, (ROWS, ROWS), 0) < lax.broadcasted_iota(
        jnp.int32, (ROWS, ROWS), 1
    )
    counts = jnp.dot(
        hits_f.astype(jnp.bfloat16),
        earlier.astype(jnp.float32).astype(jnp.bfloat16),
        preferred_element_type=jnp.float32,
    )
    ranks = jnp.sum(counts * hits_f, axis=0, keepdims=True).astype(jnp.int32)
    slots = owners * CAP + ranks
    placing = (
        (lax.broadcasted_iota(jnp.int32, (SLABS * CAP, ROWS), 0) == slots)
        .astype(jnp.float32)
        .astype(jnp.bfloat16)
    )
    rank_hits = (
        (lax.broadcasted_iota(jnp.int32, (128, ROWS), 0) % CAP == ranks)
        .astype(jnp.float32)
        .astype(jnp.bfloat16)
    )
    high = (labels // 32).astype(jnp.float32)
    low = (labels % 32 + 1).astype(jnp.float32)
    codes = jnp.concatenate([hits_f * high, hits_f * low], axis=0).astype(jnp.bfloat16)
    placed_codes = lax.dot_general(
        codes, rank_hits, (((1,), (1,)), ((), ())), preferred_element_type=jnp.float32
    )
    label_rows = placed_codes[:SLABS] * 32.0 + placed_codes[SLABS:] - 1.0
    for k in range(SLABS):
        sent_labels[core, k] = label_rows[k : k + 1, :]
    loads[2].wait()
    placed = jnp.dot(placing, values_ref[...], preferred_element_type=jnp.float32)
    sent[core] = placed.astype(jnp.bfloat16).reshape(SLABS, CAP, 128)

    def remote(src_ref, dst_ref, send_sem, recv_sem, to):
        return pltpu.make_async_remote_copy(
            src_ref=src_ref,
            dst_ref=dst_ref,
            send_sem=send_sem,
            recv_sem=recv_sem,
            device_id=to,
            device_id_type=MESH,
        )

    def arrived(ref, sem):
        pltpu.make_async_copy(ref, ref, sem).wait()

    partner = {"slab": z * 2 + 1 - core}
    hand_values = remote(sent.at[0], sent.at[0], hand_sem.at[0], hand_sem.at[1], partner)
    hand_labels = remote(
        sent_labels.at[0], sent_labels.at[0], hand_sem.at[2], hand_sem.at[3], partner
    )
    own_block = green.at[z * 2 + 1]
    own_copy = remote(own_block, own_block, own_sem.at[0], own_sem.at[1], partner)

    def green_copy(block, piece, d):
        ref = green.at[block * 2 + piece // 2, piece % 2]
        return remote(ref, ref, green_send, green_recv.at[block, piece], {"slab": slab + 2 * d})

    def pair_copy(block, piece):
        ref = green.at[block * 2 + piece // 2, piece % 2]
        return remote(ref, ref, pair_send, pair_recv.at[block], partner)

    def green_wait(block, piece):
        arrived(green.at[block * 2 + piece // 2, piece % 2], green_recv.at[block, piece])

    def green_start(piece):
        @pl.when(z < CHIPS - 1)
        def _():
            green_copy(z, piece, 1).start()

        @pl.when(z > 0)
        def _():
            green_copy(z, piece, -1).start()

    def green_step(step):
        for piece in range(4):

            @pl.when(z >= step)
            def _():
                green_wait(z - step, piece)

                @pl.when(z < CHIPS - 1)
                def _():
                    green_copy(z - step, piece, 1).start()

                pair_copy(z - step, piece).start()

            @pl.when(z + step < CHIPS)
            def _():
                green_wait(z + step, piece)

                @pl.when(z > 0)
                def _():
                    green_copy(z + step, piece, -1).start()

                pair_copy(z + step, piece).start()

    def trace_send(chip):
        to = {"slab": chip * 2 + core}
        owners_of = pl.ds(chip * 2, 2)
        remote(sent.at[:, owners_of], got.at[z], trace_sem.at[0], trace_sem.at[1], to).start()
        remote(
            sent_labels.at[:, owners_of], got_labels.at[z], trace_sem.at[2], trace_sem.at[3], to
        ).start()

    def all_traces(i):
        arrived((got, got_labels)[i // 2].at[pl.ds(0, CHIPS - 1)], trace_sem.at[i])

    def trace_steps(first, last):
        for s in range(first, last + 1):

            @pl.when(z >= s)
            def _():
                if s > 1:
                    pl.semaphore_wait(from_left.at[s - 2], 1)

                @pl.when(z < CHIPS - 1)
                def _():
                    pl.semaphore_signal(
                        from_left.at[s - 1], inc=1, device_id=along(1), device_id_type=MESH
                    )

                trace_send(z - s)

            @pl.when(z + s < CHIPS)
            def _():
                if s > 1:
                    pl.semaphore_wait(from_right.at[s - 2], 1)

                @pl.when(z > 0)
                def _():
                    pl.semaphore_signal(
                        from_right.at[s - 1], inc=1, device_id=along(-1), device_id_type=MESH
                    )

                trace_send(z + s)

    gap = jnp.where(h == 0, CHIPS - 1 - z, z)
    inward = 1 - 2 * h

    def other_line():
        pl.semaphore_wait(across, 1)

        @pl.when(gap < CHIPS - 1)
        def _():
            pl.semaphore_signal(across, inc=1, device_id=along(-inward), device_id_type=MESH)

    def block_of(half, a, b, hh):
        return at(a, b, hh) if half == 0 else at(b, a, hh)

    def res_copy(half, a, b, hh, quarter, way, sem):
        first = half * ROWS + max(quarter, 0) * (ROWS // 2)
        count = ROWS if quarter < 0 else ROWS // 2
        ref = res.at[block_of(half, a, b, hh), pl.ds(first, count), :]
        to = {"src": block_of(half, way[0], way[1], h)}
        remote(ref, ref, res_send, res_recv.at[sem], to).start()

    def give(turn, a, b):
        ref = res.at[at(a, b, (h, 1 - h)[turn]), pl.ds(0, ROWS), :]
        remote(ref, ref, give_send, give_recv.at[turn], partner).start()

    RIGHT, LEFT, UP, DOWN = (1, 0), (-1, 0), (0, 1), (0, -1)

    def res_round(step, turn):
        hh = (h, 1 - h)[turn]
        for half in range(2):

            def sem(number):
                return (turn * 5 + number - 1) * 2 + half

            if step > 0:
                ref = (
                    res.at[0],
                    res.at[0, pl.ds(0, ROWS), :],
                    res.at[pl.ds(0, 3)],
                    res.at[0],
                    res.at[pl.ds(0, 2)],
                )[step - 1]
                arrived(ref, res_recv.at[sem(step)])
            if step == 0:
                res_copy(half, 0, 0, hh, -1, RIGHT, sem(1))
                res_copy(half, 0, 0, hh, -1, LEFT, sem(1))
            elif step == 1:
                res_copy(half, -1, 0, hh, 0, RIGHT, sem(2))
                res_copy(half, 1, 0, hh, 1, LEFT, sem(2))
            elif step == 3:
                for a in (0, -1, 1):
                    res_copy(half, a, -1, hh, 0, UP, sem(5))
                    res_copy(half, a, 1, hh, 1, DOWN, sem(5))
            elif step == 4:
                res_copy(half, 2, -1, hh, 0, UP, sem(5))
                res_copy(half, 2, 1, hh, 1, DOWN, sem(5))
        if step < 3:
            for half in range(2):
                number = (turn * 5 + (3 if step < 2 else 4) - 1) * 2 + half
                for a in ((0,), (-1, 1), (2,))[step]:
                    res_copy(half, a, 0, hh, -1, UP, number)
                    res_copy(half, a, 0, hh, -1, DOWN, number)
        for a, b in (
            ((0, 0),),
            ((-1, 0), (1, 0)),
            ((2, 0),),
            ((0, -1), (0, 1), (-1, -1), (-1, 1), (1, -1), (1, 1)),
            ((2, -1), (2, 1)),
            ((0, 2), (-1, 2), (1, 2), (2, 2)),
        )[step]:
            give(turn, a, b)

    loads[3].wait()
    pl.semaphore_wait(barrier, len(neighbours))

    @pl.when(core == 0)
    def _():
        hand_labels.start()
        hand_values.start()
        for piece in range(2):
            green_start(piece)
        arrived(own_block, own_sem.at[1])
        for piece in range(2, 4):
            green_start(piece)
        for piece in range(2):
            pair_copy(z, piece).start()
        for step in range(1, EARLY_STEPS + 1):
            green_step(step)
        for turn in range(2):
            arrived(res.at[pl.ds(0, SRCS // 4)], give_recv.at[turn])

    @pl.when(core == 1)
    def _():
        own_copy.start()
        arrived(sent_labels.at[0], hand_sem.at[3])
        arrived(sent.at[0], hand_sem.at[1])
        trace_steps(1, CHIPS - 1)
        for i in range(2):
            got[z, i] = sent[i, pl.ds(z * 2, 2)]
            got_labels[z, i] = sent_labels[i, pl.ds(z * 2, 2)]

        @pl.when(gap == 0)
        def _():
            pl.semaphore_signal(across, inc=1, device_id=along(inward), device_id_type=MESH)

        @pl.when(gap <= 4)
        def _():
            other_line()

        all_traces(3)
        all_traces(1)

        @pl.when(gap > 4)
        def _():
            other_line()

        low_lanes = lax.broadcasted_iota(jnp.int32, (1, 128), 1) < CAP
        rows_f = lax.broadcasted_iota(jnp.int32, (ROWS, 128), 0).astype(jnp.float32)
        for owner in range(2):
            picks = []
            for chip in range(CHIPS):
                row = jnp.where(low_lanes, got_labels[chip, 0, owner], got_labels[chip, 1, owner])
                picks.append((rows_f == row).astype(jnp.float32).astype(jnp.bfloat16))
            assembled = jnp.dot(
                jnp.concatenate(picks, axis=1),
                got[:, :, owner].reshape(SLABS * CAP, 128),
                preferred_element_type=jnp.float32,
            )
            res[src, pl.ds(owner * ROWS, ROWS), :] = assembled.astype(jnp.bfloat16)

        twin = at(0, 0, 1 - h)
        twin_copy = remote(
            res.at[src], res.at[src], twin_sem.at[0], twin_sem.at[1], {"src": twin}
        )
        twin_copy.start()
        for step in range(5):
            res_round(step, 0)
        arrived(res.at[twin], twin_sem.at[1])
        res_round(0, 1)
        res_round(5, 0)
        for step in range(1, 6):
            res_round(step, 1)
        twin_copy.wait_send()

    acc_re[...] = jnp.zeros_like(acc_re)
    acc_im[...] = jnp.zeros_like(acc_im)
    loads[4].wait()

    def chip_of(n):
        m = jnp.minimum(z, CHIPS - 1 - z)
        side = z + jnp.where(n % 2 == 1, -((n + 1) // 2), n // 2)
        rest = jnp.where(z < CHIPS // 2, n, CHIPS - 1 - n)
        return jnp.where(n <= 2 * m, side, rest)

    def multiply(n, carry):
        block = chip_of(n)
        far = jnp.abs(block - z)
        before = jnp.abs(chip_of(jnp.maximum(n - 1, 0)) - z)

        @pl.when((core == 0) & (far > EARLY_STEPS) & (far > before))
        def _():
            green_step(far)

        @pl.when((core == 1) & (far == 0))
        def _():
            arrived(green.at[0], pair_recv.at[block])

        @pl.when((core == 1) & (far > 0))
        def _():
            arrived(green.at[pl.ds(0, 2)], pair_recv.at[block])

        for i in range(2):
            index = block * 2 + i
            rows = pl.ds(pl.multiple_of(core * ROWS, ROWS), ROWS)
            left = jnp.concatenate([res[2 * index, rows, :], res[2 * index + 1, rows, :]], axis=1)
            g_re = green[index, 0]
            g_im = green[index, 1]
            right_re = jnp.concatenate([g_re[:CAP], g_im[:CAP], g_re[CAP:], g_im[CAP:]], axis=0)
            right_im = jnp.concatenate([g_im[:CAP], -g_re[:CAP], g_im[CAP:], -g_re[CAP:]], axis=0)
            acc_re[...] += jnp.dot(left, right_re, preferred_element_type=jnp.float32)
            acc_im[...] += jnp.dot(left, right_im, preferred_element_type=jnp.float32)
        return carry

    lax.fori_loop(0, CHIPS, multiply, 0)
    partial = jnp.sum(
        fields[0].astype(jnp.float32) * acc_re[...] - fields[1].astype(jnp.float32) * acc_im[...],
        axis=0,
        keepdims=True,
    )
    parts[slab] = partial
    for d in range(1, SLABS):
        to = {"slab": (slab + d) % SLABS}
        remote(parts.at[slab], parts.at[slab], sum_sem.at[0], sum_sem.at[1], to).start()

    end = (z == 0) | (z == CHIPS - 1)

    @pl.when(core == 0)
    def _():
        hand_values.wait_send()
        hand_labels.wait_send()
        arrived(green.at[pl.ds(0, SLABS - 1)], pair_send)

        @pl.when(end)
        def _():
            arrived(res.at[pl.ds(0, 2)], green_send)

        @pl.when(jnp.logical_not(end))
        def _():
            arrived(res.at[pl.ds(0, 2 * CHIPS + 2)], green_send)

    @pl.when(core == 1)
    def _():
        own_copy.wait_send()
        all_traces(0)
        all_traces(2)
        arrived(res.at[pl.ds(0, SRCS - 2)], res_send)
        arrived(res.at[pl.ds(0, SRCS // 2)], give_send)

    arrived(parts.at[pl.ds(0, SLABS - 1)], sum_sem.at[1])
    out_ref[...] = jnp.sum(parts[...], axis=0)
    arrived(parts.at[pl.ds(0, SLABS - 1)], sum_sem.at[0])


def on_device(trace_values, trace_owner, trace_source, source_fields, green_fields):
    dma = pltpu.SemaphoreType.DMA
    out = pl.pallas_call(
        kernel,
        out_shape=jax.ShapeDtypeStruct((1, CELLS), jnp.float32),
        in_specs=[pl.BlockSpec(memory_space=pltpu.HBM)] * 5,
        out_specs=pl.BlockSpec(memory_space=pltpu.VMEM),
        scratch_shapes=[
            pltpu.VMEM((1, ROWS), jnp.int32),
            pltpu.VMEM((1, ROWS), jnp.int32),
            pltpu.VMEM((ROWS, 128), jnp.bfloat16),
            pltpu.VMEM((2, SLABS, CAP, 128), jnp.bfloat16),
            pltpu.VMEM((2, SLABS, 1, 128), jnp.float32),
            pltpu.VMEM((CHIPS, 2, 2, CAP, 128), jnp.bfloat16),
            pltpu.VMEM((CHIPS, 2, 2, 1, 128), jnp.float32),
            pltpu.VMEM((SRCS, 2 * ROWS, 128), jnp.bfloat16),
            pltpu.VMEM((SLABS, 2, 128, CELLS), jnp.bfloat16),
            pltpu.VMEM((2, ROWS, CELLS), jnp.bfloat16),
            pltpu.VMEM((ROWS, CELLS), jnp.float32),
            pltpu.VMEM((ROWS, CELLS), jnp.float32),
            pltpu.VMEM((SLABS, 1, CELLS), jnp.float32),
            dma((5,)),
            dma((4,)),
            dma((4,)),
            dma,
            dma((CHIPS, 4)),
            dma,
            dma((CHIPS,)),
            dma((2,)),
            dma((2,)),
            dma,
            dma((20,)),
            dma,
            dma((2,)),
            dma((2,)),
            pltpu.SemaphoreType.REGULAR((CHIPS - 1,)),
            pltpu.SemaphoreType.REGULAR((CHIPS - 1,)),
            pltpu.SemaphoreType.REGULAR,
        ],
        compiler_params=pltpu.CompilerParams(
            collective_id=0, has_side_effects=True, vmem_limit_bytes=60 * 1024 * 1024
        ),
    )(
        trace_owner.reshape(1, ROWS),
        trace_source.reshape(1, ROWS),
        trace_values[0],
        source_fields,
        green_fields,
    )
    return out.reshape(CELLS)


def solution(mesh):
    in_specs = (
        P("src", "slab", None),
        P("src", "slab", None),
        P("src", "slab"),
        P(None, "slab", "src"),
        P(None, "slab", "src"),
    )
    return jax.shard_map(
        on_device, mesh=mesh, in_specs=in_specs, out_specs=P("src"), check_vma=False
    )
```

time: 89.6 us -> 83.4 us (0.931)
  Pallas kernels: 88.2 us -> 82 us
    pallas_call x1, Pallas kernels: 88.2 us -> 82 us  [on_device(): pl.pallas_call(kernel, out_shape=jax.ShapeDtypeStruct((1, CELLS), jnp.flo...]
where the time goes in v3:
time: 83.4 us; the launch traced here: 83.3 us
  Pallas kernels  82 us (98%)
  local copies, waits for them, and re-layouts  1.26 us (2%)
    pallas_call x1, Pallas kernels, on_device(): pl.pallas_call(kernel, out_shape=jax.ShapeDtypeStruct((1, CELLS), jnp.flo...  82 us

profile of v3, /device:TPU:1, one launch (start us, length us, event | category | flops | bytes accessed | tf_op | source)
XLA Modules:
  0.0 83.3 jit_solution(10035576128503955503)
XLA Ops:
  0.0 82.0 %shard_map.55 = f32[1,512]{1,0:T(1,128)} custom-call(s32[1,512]{1,0:T(1,128)} %bitcast.5, s32[1,512]{1,0:T(1,128)} %label_hbm.1, bf16[512,128]{1,0:T(8,128)(2,1)} %bitcast.3, bf16[2,512,512]{2,1,0:T(8,128)(2,1)} %fields_hbm.1, bf16[2,128,512]{2,1,0:T(8,128)(2,1)} %green_hbm.1), custom_call_target="tpu_custom_call" | custom-call | tf_op jit(solution)/shard_map/pallas_call | solution.py:458
  82.0 1.3 %copy.7 = f32[512]{0:T(512)} copy(f32[512]{0:T(512)} %bitcast.4) | data formatting | bytes 4096

commit v4 on v3

v4 whole, which is shorter than its diff:
```python
import jax
import jax.numpy as jnp
from jax import lax
from jax.experimental import pallas as pl
from jax.experimental.pallas import tpu as pltpu
from jax.sharding import PartitionSpec as P

MESH = pl.DeviceIdType.MESH
SLABS = 16
SRCS = 32
CAP = 64
ROWS = 512
CELLS = 512
CHIPS = 8
RING = 16
EARLY_STEPS = 6
PART = ROWS // 2
ROUNDS = ((1, 0), (1, 1), (2, 0), (2, 1), (3, 0), (3, 1), (4, 0), (4, 1), (0, 2), (5, 0), (5, 1), (1, 2), (2, 2))
ROUNDS += ((0, 3), (3, 2), (1, 3), (4, 2), (2, 3), (5, 2), (3, 3), (4, 3), (5, 3))


def kernel(
    owner_hbm,
    label_hbm,
    values_hbm,
    fields_hbm,
    green_hbm,
    parts,
    owner_ref,
    label_ref,
    values_ref,
    sent,
    sent_labels,
    got,
    got_labels,
    gathered,
    res,
    green,
    fields,
    acc_re,
    acc_im,
    load_sem,
    hand_sem,
    trace_sem,
    trace_recv,
    label_recv,
    green_send,
    green_recv,
    pair_send,
    pair_recv,
    own_sem,
    twin_send,
    twin_recv,
    res_send,
    res_recv,
    give_send,
    give_recv,
    sum_sem,
    from_left,
    from_right,
    across,
):
    slab = lax.axis_index("slab")
    src = lax.axis_index("src")
    z, core = slab // 2, slab % 2
    y, x, h = src // 8, (src // 2) % 4, src % 2
    ring = h * CHIPS + z

    loads = []
    for i, (a, b) in enumerate(
        (
            (owner_hbm, owner_ref),
            (label_hbm, label_ref),
            (values_hbm, values_ref),
            (green_hbm, green.at[slab]),
            (fields_hbm, fields),
        )
    ):
        loads.append(pltpu.make_async_copy(a, b, load_sem.at[i]))
        loads[-1].start()

    def at(dx, dy, hh):
        return (((y + dy + 4) % 4) * 4 + (x + dx + 4) % 4) * 2 + hh

    def along(d, to_core=core):
        to = (ring + d + RING) % RING
        return {"slab": (to % CHIPS) * 2 + to_core, "src": src - h + to // CHIPS}

    gap = jnp.where(h == 0, CHIPS - 1 - z, z)
    inward = 1 - 2 * h
    barrier = pltpu.get_barrier_semaphore()

    def greet(other):
        pl.semaphore_signal(barrier, inc=1, device_id=other, device_id_type=MESH)

    greet({"slab": z * 2 + 1 - core})

    @pl.when(z > 0)
    def _():
        greet(along(-1))

    @pl.when(z < CHIPS - 1)
    def _():
        greet(along(1))

    @pl.when(core == 1)
    def _():
        for dx, dy in ((1, 0), (-1, 0), (0, 1), (0, -1)):
            greet({"src": at(dx, dy, h)})

        @pl.when(gap == 0)
        def _():
            greet(along(inward, 0))

    greeted = 1 + (z > 0).astype(jnp.int32) + (z < CHIPS - 1).astype(jnp.int32)
    greeted += jnp.where(core == 1, 4, (gap == 0).astype(jnp.int32))

    def remote(src_ref, dst_ref, send_sem, recv_sem, to):
        return pltpu.make_async_remote_copy(
            src_ref=src_ref,
            dst_ref=dst_ref,
            send_sem=send_sem,
            recv_sem=recv_sem,
            device_id=to,
            device_id_type=MESH,
        )

    def arrived(ref, sem):
        pltpu.make_async_copy(ref, ref, sem).wait()

    partner = {"slab": z * 2 + 1 - core}
    hand_values = remote(sent.at[0], sent.at[0], hand_sem.at[0], hand_sem.at[1], partner)
    hand_labels = remote(
        sent_labels.at[0], sent_labels.at[0], hand_sem.at[2], hand_sem.at[3], partner
    )
    own_block = green.at[z * 2 + 1]
    own_copy = remote(green_hbm, own_block, own_sem.at[0], own_sem.at[1], partner)

    def place_traces():
        loads[0].wait()
        loads[1].wait()
        owners = owner_ref[...]
        labels = label_ref[...]
        hits = lax.broadcasted_iota(jnp.int32, (SLABS, ROWS), 0) == owners
        hits_f = hits.astype(jnp.float32)
        earlier = lax.broadcasted_iota(jnp.int32, (ROWS, ROWS), 0) < lax.broadcasted_iota(
            jnp.int32, (ROWS, ROWS), 1
        )
        counts = jnp.dot(
            hits_f.astype(jnp.bfloat16),
            earlier.astype(jnp.float32).astype(jnp.bfloat16),
            preferred_element_type=jnp.float32,
        )
        ranks = jnp.sum(counts * hits_f, axis=0, keepdims=True).astype(jnp.int32)
        slots = owners * CAP + ranks
        placing = (
            (lax.broadcasted_iota(jnp.int32, (SLABS * CAP, ROWS), 0) == slots)
            .astype(jnp.float32)
            .astype(jnp.bfloat16)
        )
        rank_hits = (
            (lax.broadcasted_iota(jnp.int32, (128, ROWS), 0) % CAP == ranks)
            .astype(jnp.float32)
            .astype(jnp.bfloat16)
        )
        high = (labels // 32).astype(jnp.float32)
        low = (labels % 32 + 1).astype(jnp.float32)
        codes = jnp.concatenate([hits_f * high, hits_f * low], axis=0).astype(jnp.bfloat16)
        placed_codes = lax.dot_general(
            codes, rank_hits, (((1,), (1,)), ((), ())), preferred_element_type=jnp.float32
        )
        label_rows = placed_codes[:SLABS] * 32.0 + placed_codes[SLABS:] - 1.0
        for k in range(SLABS):
            sent_labels[core, k] = label_rows[k : k + 1, :]
        loads[2].wait()
        placed = jnp.dot(placing, values_ref[...], preferred_element_type=jnp.float32)
        sent[core] = placed.astype(jnp.bfloat16).reshape(SLABS, CAP, 128)

    def green_copy(block, piece, d, source=None):
        ref = green.at[block * 2 + piece // 2, piece % 2]
        to = {"slab": slab + 2 * d}
        return remote(source or ref, ref, green_send, green_recv.at[block, piece], to)

    def pair_copy(block, piece):
        ref = green.at[block * 2 + piece // 2, piece % 2]
        return remote(ref, ref, pair_send, pair_recv.at[block], partner)

    def green_wait(block, piece):
        arrived(green.at[block * 2 + piece // 2, piece % 2], green_recv.at[block, piece])

    def green_start(piece):
        source = green_hbm.at[piece] if piece < 2 else None

        @pl.when(z < CHIPS - 1)
        def _():
            green_copy(z, piece, 1, source).start()

        @pl.when(z > 0)
        def _():
            green_copy(z, piece, -1, source).start()

    def green_step(step):
        for piece in range(4):

            @pl.when(z >= step)
            def _():
                green_wait(z - step, piece)

                @pl.when(z < CHIPS - 1)
                def _():
                    green_copy(z - step, piece, 1).start()

                pair_copy(z - step, piece).start()

            @pl.when(z + step < CHIPS)
            def _():
                green_wait(z + step, piece)

                @pl.when(z > 0)
                def _():
                    green_copy(z + step, piece, -1).start()

                pair_copy(z + step, piece).start()

    def trace_send(chip):
        to = {"slab": chip * 2 + core}
        owners_of = pl.ds(chip * 2, 2)
        remote(sent.at[:, owners_of], got.at[z], trace_sem.at[0], trace_recv.at[z], to).start()
        remote(
            sent_labels.at[:, owners_of], got_labels.at[z], trace_sem.at[1], label_recv.at[z], to
        ).start()

    def all_traces(i):
        arrived((got, got_labels)[i].at[pl.ds(0, CHIPS - 1)], trace_sem.at[i])

    def assemble(chip, first):
        low_lanes = lax.broadcasted_iota(jnp.int32, (1, 128), 1) < CAP
        rows_f = lax.broadcasted_iota(jnp.int32, (ROWS, 128), 0).astype(jnp.float32)
        for owner in range(2):
            row = jnp.where(low_lanes, got_labels[chip, 0, owner], got_labels[chip, 1, owner])
            picks = (rows_f == row).astype(jnp.float32).astype(jnp.bfloat16)
            term = jnp.dot(
                picks, got[chip, :, owner].reshape(128, 128), preferred_element_type=jnp.float32
            )
            gathered[owner] = term if first else gathered[owner] + term

    def chip_of(n):
        m = jnp.minimum(z, CHIPS - 1 - z)
        side = z + jnp.where(n % 2 == 1, -((n + 1) // 2), n // 2)
        rest = jnp.where(z < CHIPS // 2, n, CHIPS - 1 - n)
        return jnp.where(n <= 2 * m, side, rest)

    def trace_steps(first, last):
        for s in range(first, last + 1):

            @pl.when(z >= s)
            def _():
                if s > 1:
                    pl.semaphore_wait(from_left.at[s - 2], 1)

                @pl.when(z < CHIPS - 1)
                def _():
                    pl.semaphore_signal(
                        from_left.at[s - 1], inc=1, device_id=along(1), device_id_type=MESH
                    )

                trace_send(z - s)

            @pl.when(z + s < CHIPS)
            def _():
                if s > 1:
                    pl.semaphore_wait(from_right.at[s - 2], 1)

                @pl.when(z > 0)
                def _():
                    pl.semaphore_signal(
                        from_right.at[s - 1], inc=1, device_id=along(-1), device_id_type=MESH
                    )

                trace_send(z + s)

    def other_line():
        pl.semaphore_wait(across, 1)

        @pl.when(gap < CHIPS - 1)
        def _():
            pl.semaphore_signal(across, inc=1, device_id=along(-inward), device_id_type=MESH)

    def block_of(half, a, b, hh):
        return at(a, b, hh) if half == 0 else at(b, a, hh)

    def res_copy(half, a, b, hh, chunk, quarter, way, sem):
        first = half * ROWS + chunk * PART + max(quarter, 0) * (PART // 2)
        count = PART if quarter < 0 else PART // 2
        ref = res.at[block_of(half, a, b, hh), pl.ds(first, count), :]
        to = {"src": block_of(half, way[0], way[1], h)}
        remote(ref, ref, res_send, res_recv.at[sem], to).start()

    def give(turn, a, b):
        ref = res.at[at(a, b, (h, 1 - h)[turn // 2]), pl.ds(turn % 2 * PART, PART), :]
        remote(ref, ref, give_send, give_recv.at[turn], partner).start()

    RIGHT, LEFT, UP, DOWN = (1, 0), (-1, 0), (0, 1), (0, -1)

    def res_round(step, turn):
        hh, chunk = (h, 1 - h)[turn // 2], turn % 2
        for half in range(2):

            def sem(number):
                return (turn * 5 + number - 1) * 2 + half

            if step > 0:
                ref = (
                    res.at[0, pl.ds(0, ROWS), :],
                    res.at[0, pl.ds(0, PART), :],
                    res.at[pl.ds(0, 3), pl.ds(0, ROWS), :],
                    res.at[0, pl.ds(0, ROWS), :],
                    res.at[0],
                )[step - 1]
                arrived(ref, res_recv.at[sem(step)])
            if step == 0:
                res_copy(half, 0, 0, hh, chunk, -1, RIGHT, sem(1))
                res_copy(half, 0, 0, hh, chunk, -1, LEFT, sem(1))
            elif step == 1:
                res_copy(half, -1, 0, hh, chunk, 0, RIGHT, sem(2))
                res_copy(half, 1, 0, hh, chunk, 1, LEFT, sem(2))
            elif step == 3:
                for a in (0, -1, 1):
                    res_copy(half, a, -1, hh, chunk, 0, UP, sem(5))
                    res_copy(half, a, 1, hh, chunk, 1, DOWN, sem(5))
            elif step == 4:
                res_copy(half, 2, -1, hh, chunk, 0, UP, sem(5))
                res_copy(half, 2, 1, hh, chunk, 1, DOWN, sem(5))
        if step < 3:
            for half in range(2):
                number = (turn * 5 + (3 if step < 2 else 4) - 1) * 2 + half
                for a in ((0,), (-1, 1), (2,))[step]:
                    res_copy(half, a, 0, hh, chunk, -1, UP, number)
                    res_copy(half, a, 0, hh, chunk, -1, DOWN, number)
        for a, b in (
            ((0, 0),),
            ((-1, 0), (1, 0)),
            ((2, 0),),
            ((0, -1), (0, 1), (-1, -1), (-1, 1), (1, -1), (1, 1)),
            ((2, -1), (2, 1)),
            ((0, 2), (-1, 2), (1, 2), (2, 2)),
        )[step]:
            give(turn, a, b)

    @pl.when(core == 0)
    def _():
        pl.semaphore_wait(barrier, greeted)
        for piece in range(2):
            green_start(piece)

    @pl.when(core == 1)
    def _():
        pl.semaphore_wait(barrier, greeted)
        own_copy.start()

    place_traces()
    loads[3].wait()

    @pl.when(core == 0)
    def _():
        hand_labels.start()
        hand_values.start()
        arrived(own_block, own_sem.at[1])
        for piece in range(2, 4):
            green_start(piece)
        for piece in range(2):
            pair_copy(z, piece).start()
        for step in range(1, EARLY_STEPS + 1):
            if step == 2:

                @pl.when(gap == 0)
                def _():
                    pl.semaphore_wait(across, 1)
                    pl.semaphore_signal(
                        across, inc=1, device_id=along(inward, 1), device_id_type=MESH
                    )

            green_step(step)
        for turn in range(4):
            arrived(res.at[pl.ds(0, SRCS // 8)], give_recv.at[turn])

    @pl.when(core == 1)
    def _():
        arrived(sent_labels.at[0], hand_sem.at[3])
        arrived(sent.at[0], hand_sem.at[1])
        trace_steps(1, CHIPS - 1)
        for i in range(2):
            got[z, i] = sent[i, pl.ds(z * 2, 2)]
            got_labels[z, i] = sent_labels[i, pl.ds(z * 2, 2)]

        @pl.when(gap == 0)
        def _():
            pl.semaphore_signal(across, inc=1, device_id=partner, device_id_type=MESH)

        @pl.when(gap <= 4)
        def _():
            other_line()

        assemble(z, True)

        def next_chip(n, carry):
            chip = chip_of(n)
            arrived(got_labels.at[chip], label_recv.at[chip])
            arrived(got.at[chip], trace_recv.at[chip])
            assemble(chip, False)
            return carry

        lax.fori_loop(1, CHIPS, next_chip, 0)
        for owner in range(2):
            res[src, pl.ds(owner * ROWS, ROWS), :] = gathered[owner].astype(jnp.bfloat16)

        res_round(0, 0)
        res_round(0, 1)

        @pl.when(gap > 4)
        def _():
            other_line()

        twin = at(0, 0, 1 - h)
        for chunk in range(2):
            for half in range(2):
                ref = res.at[src, pl.ds(half * ROWS + chunk * PART, PART), :]
                remote(ref, ref, twin_send, twin_recv.at[chunk], {"src": twin}).start()
        for step, turn in ROUNDS:
            if step == 0:
                arrived(res.at[0, pl.ds(0, ROWS), :], twin_recv.at[turn - 2])
            res_round(step, turn)
        arrived(res.at[0], twin_send)

    acc_re[...] = jnp.zeros_like(acc_re)
    acc_im[...] = jnp.zeros_like(acc_im)
    loads[4].wait()

    def multiply(n, carry):
        block = chip_of(n)
        far = jnp.abs(block - z)
        before = jnp.abs(chip_of(jnp.maximum(n - 1, 0)) - z)

        @pl.when((core == 0) & (far > EARLY_STEPS) & (far > before))
        def _():
            green_step(far)

        @pl.when((core == 1) & (far == 0))
        def _():
            arrived(green.at[0], pair_recv.at[block])

        @pl.when((core == 1) & (far > 0))
        def _():
            arrived(green.at[pl.ds(0, 2)], pair_recv.at[block])

        for i in range(2):
            index = block * 2 + i
            rows = pl.ds(pl.multiple_of(core * ROWS, ROWS), ROWS)
            left = jnp.concatenate([res[2 * index, rows, :], res[2 * index + 1, rows, :]], axis=1)
            g_re = green[index, 0]
            g_im = green[index, 1]
            right_re = jnp.concatenate([g_re[:CAP], g_im[:CAP], g_re[CAP:], g_im[CAP:]], axis=0)
            right_im = jnp.concatenate([g_im[:CAP], -g_re[:CAP], g_im[CAP:], -g_re[CAP:]], axis=0)
            acc_re[...] += jnp.dot(left, right_re, preferred_element_type=jnp.float32)
            acc_im[...] += jnp.dot(left, right_im, preferred_element_type=jnp.float32)
        return carry

    lax.fori_loop(0, CHIPS, multiply, 0)
    partial = jnp.sum(
        fields[0].astype(jnp.float32) * acc_re[...] - fields[1].astype(jnp.float32) * acc_im[...],
        axis=0,
        keepdims=True,
    )
    parts[slab] = partial
    for d in range(1, SLABS):
        to = {"slab": (slab + d) % SLABS}
        remote(parts.at[slab], parts.at[slab], sum_sem.at[0], sum_sem.at[1], to).start()

    end = (z == 0) | (z == CHIPS - 1)

    @pl.when(core == 0)
    def _():
        hand_values.wait_send()
        hand_labels.wait_send()
        arrived(green.at[pl.ds(0, SLABS - 1)], pair_send)

        @pl.when(end)
        def _():
            arrived(res.at[pl.ds(0, 2)], green_send)

        @pl.when(jnp.logical_not(end))
        def _():
            arrived(res.at[pl.ds(0, 2 * CHIPS + 2)], green_send)

    @pl.when(core == 1)
    def _():
        own_copy.wait_send()
        all_traces(0)
        all_traces(1)
        arrived(res.at[pl.ds(0, SRCS - 2)], res_send)
        arrived(res.at[pl.ds(0, SRCS // 2)], give_send)

    arrived(parts.at[pl.ds(0, SLABS - 1)], sum_sem.at[1])
    arrived(parts.at[pl.ds(0, SLABS - 1)], sum_sem.at[0])


def total(parts_ref, out_ref):
    out_ref[...] = jnp.sum(parts_ref[...], axis=0)


def on_device(trace_values, trace_owner, trace_source, source_fields, green_fields):
    dma = pltpu.SemaphoreType.DMA
    vmem = pl.BlockSpec(memory_space=pltpu.VMEM)
    parts = pl.pallas_call(
        kernel,
        out_shape=jax.ShapeDtypeStruct((SLABS, 1, CELLS), jnp.float32),
        in_specs=[pl.BlockSpec(memory_space=pltpu.HBM)] * 5,
        out_specs=vmem,
        scratch_shapes=[
            pltpu.VMEM((1, ROWS), jnp.int32),
            pltpu.VMEM((1, ROWS), jnp.int32),
            pltpu.VMEM((ROWS, 128), jnp.bfloat16),
            pltpu.VMEM((2, SLABS, CAP, 128), jnp.bfloat16),
            pltpu.VMEM((2, SLABS, 1, 128), jnp.float32),
            pltpu.VMEM((CHIPS, 2, 2, CAP, 128), jnp.bfloat16),
            pltpu.VMEM((CHIPS, 2, 2, 1, 128), jnp.float32),
            pltpu.VMEM((2, ROWS, 128), jnp.float32),
            pltpu.VMEM((SRCS, 2 * ROWS, 128), jnp.bfloat16),
            pltpu.VMEM((SLABS, 2, 128, CELLS), jnp.bfloat16),
            pltpu.VMEM((2, ROWS, CELLS), jnp.bfloat16),
            pltpu.VMEM((ROWS, CELLS), jnp.float32),
            pltpu.VMEM((ROWS, CELLS), jnp.float32),
            dma((5,)),
            dma((4,)),
            dma((2,)),
            dma((CHIPS,)),
            dma((CHIPS,)),
            dma,
            dma((CHIPS, 4)),
            dma,
            dma((CHIPS,)),
            dma((2,)),
            dma,
            dma((2,)),
            dma,
            dma((40,)),
            dma,
            dma((4,)),
            dma((2,)),
            pltpu.SemaphoreType.REGULAR((CHIPS - 1,)),
            pltpu.SemaphoreType.REGULAR((CHIPS - 1,)),
            pltpu.SemaphoreType.REGULAR,
        ],
        compiler_params=pltpu.CompilerParams(
            collective_id=0, has_side_effects=True, vmem_limit_bytes=60 * 1024 * 1024
        ),
    )(
        trace_owner.reshape(1, ROWS),
        trace_source.reshape(1, ROWS),
        trace_values[0],
        source_fields,
        green_fields,
    )
    out = pl.pallas_call(
        total,
        out_shape=jax.ShapeDtypeStruct((1, CELLS), jnp.float32),
        in_specs=[vmem],
        out_specs=vmem,
    )(parts)
    return out.reshape(CELLS)


def solution(mesh):
    in_specs = (
        P("src", "slab", None),
        P("src", "slab", None),
        P("src", "slab"),
        P(None, "slab", "src"),
        P(None, "slab", "src"),
    )
    return jax.shard_map(
        on_device, mesh=mesh, in_specs=in_specs, out_specs=P("src"), check_vma=False
    )
```

time: 83.4 us -> 80.7 us (0.968)
  Pallas kernels: 82 us -> 80.5 us
  local copies, waits for them, and re-layouts: 1.26 us -> 0 us
    pallas_call x1 -> x2, Pallas kernels: 82 us -> 80.5 us  [the longest x1 79.2 us: on_device(): pl.pallas_call(kernel, out_shape=jax.ShapeDtypeStruct((SLABS, 1, CELLS),...]
    unnamed x1 -> x0, local copies, waits for them, and re-layouts: 1.26 us -> none
where the time goes in v4:
time: 80.7 us; the launch traced here: 80.5 us
  Pallas kernels  80.5 us (100%)
    pallas_call x1, Pallas kernels, on_device(): pl.pallas_call(kernel, out_shape=jax.ShapeDtypeStruct((SLABS, 1, CELLS),...  79.2 us

profile of v4, /device:TPU:1, one launch (start us, length us, event | category | flops | bytes accessed | tf_op | source)
XLA Modules:
  0.0 80.5 jit_solution(12339508492895032833)
XLA Ops:
  0.0 79.2 %shard_map.55.parts_ref = f32[16,1,512]{2,1,0:T(1,128)} custom-call(s32[1,512]{1,0:T(1,128)} %bitcast.4, s32[1,512]{1,0:T(1,128)} %label_hbm.1, bf16[512,128]{1,0:T(8,128)(2,1)} %bitcast.3, bf16[2,512,512]{2,1,0:T(8,128)(2,1)} %fields_hbm.1, bf16[2,128,512]{2,1,0:T(8,128)(2,1)} %green_hbm.1), custom_call_target="tpu_custom_call" | custom-call | tf_op jit(solution)/shard_map/pallas_call | solution.py:514
  79.2 1.4 %shard_map.56 = f32[1,512]{1,0:T(1,128)} custom-call(f32[16,1,512]{2,1,0:T(1,128)} %shard_map.55.parts_ref), custom_call_target="tpu_custom_call" | custom-call | tf_op jit(solution)/shard_map/pallas_call | solution.py:564

commit v5 on v4

--- a/solution.py
+++ b/solution.py
@@ -453,16 +453,17 @@
         def _():
             arrived(green.at[pl.ds(0, 2)], pair_recv.at[block])
 
-        for i in range(2):
-            index = block * 2 + i
-            rows = pl.ds(pl.multiple_of(core * ROWS, ROWS), ROWS)
-            left = jnp.concatenate([res[2 * index, rows, :], res[2 * index + 1, rows, :]], axis=1)
-            g_re = green[index, 0]
-            g_im = green[index, 1]
-            right_re = jnp.concatenate([g_re[:CAP], g_im[:CAP], g_re[CAP:], g_im[CAP:]], axis=0)
-            right_im = jnp.concatenate([g_im[:CAP], -g_re[:CAP], g_im[CAP:], -g_re[CAP:]], axis=0)
-            acc_re[...] += jnp.dot(left, right_re, preferred_element_type=jnp.float32)
-            acc_im[...] += jnp.dot(left, right_im, preferred_element_type=jnp.float32)
+        rows = pl.ds(pl.multiple_of(core * ROWS, ROWS), ROWS)
+        left = jnp.concatenate([res[4 * block + i, rows, :] for i in range(4)], axis=1)
+        right_re, right_im = [], []
+        for i in range(4):
+            half = pl.ds(i % 2 * CAP, CAP)
+            g_re, g_im = (green[block * 2 + i // 2, c, half, :] for c in range(2))
+            right_re += [g_re, g_im]
+            right_im += [g_im, -g_re]
+        right_re, right_im = (jnp.concatenate(r, axis=0) for r in (right_re, right_im))
+        acc_re[...] += jnp.dot(left, right_re, preferred_element_type=jnp.float32)
+        acc_im[...] += jnp.dot(left, right_im, preferred_element_type=jnp.float32)
         return carry
 
     lax.fori_loop(0, CHIPS, multiply, 0)

time: 80.7 us -> 80.8 us (level)
  no operation moved by 1% of the time
where the time goes in v5:
time: 80.8 us; the launch traced here: 80.6 us
  Pallas kernels  80.6 us (100%)
    pallas_call x1, Pallas kernels, on_device(): pl.pallas_call(kernel, out_shape=jax.ShapeDtypeStruct((SLABS, 1, CELLS),...  79.2 us

profile of v5, /device:TPU:1, one launch (start us, length us, event | category | flops | bytes accessed | tf_op | source)
XLA Modules:
  0.0 80.6 jit_solution(2407081732650266800)
XLA Ops:
  0.0 79.2 %shard_map.55.parts_ref = f32[16,1,512]{2,1,0:T(1,128)} custom-call(s32[1,512]{1,0:T(1,128)} %bitcast.4, s32[1,512]{1,0:T(1,128)} %label_hbm.1, bf16[512,128]{1,0:T(8,128)(2,1)} %bitcast.3, bf16[2,512,512]{2,1,0:T(8,128)(2,1)} %fields_hbm.1, bf16[2,128,512]{2,1,0:T(8,128)(2,1)} %green_hbm.1), custom_call_target="tpu_custom_call" | custom-call | tf_op jit(solution)/shard_map/pallas_call | solution.py:515
  79.3 1.4 %shard_map.56 = f32[1,512]{1,0:T(1,128)} custom-call(f32[16,1,512]{2,1,0:T(1,128)} %shard_map.55.parts_ref), custom_call_target="tpu_custom_call" | custom-call | tf_op jit(solution)/shard_map/pallas_call | solution.py:565

commit v6 on v5

--- a/solution.py
+++ b/solution.py
@@ -304,20 +304,20 @@
 
     def res_round(step, turn):
         hh, chunk = (h, 1 - h)[turn // 2], turn % 2
+
+        def sem(number):
+            return turn * 5 + number - 1
+
+        if step > 0:
+            ref = (
+                res.at[0],
+                res.at[0, pl.ds(0, ROWS), :],
+                res.at[pl.ds(0, 3)],
+                res.at[0],
+                res.at[pl.ds(0, 2)],
+            )[step - 1]
+            arrived(ref, res_recv.at[sem(step)])
         for half in range(2):
-
-            def sem(number):
-                return (turn * 5 + number - 1) * 2 + half
-
-            if step > 0:
-                ref = (
-                    res.at[0, pl.ds(0, ROWS), :],
-                    res.at[0, pl.ds(0, PART), :],
-                    res.at[pl.ds(0, 3), pl.ds(0, ROWS), :],
-                    res.at[0, pl.ds(0, ROWS), :],
-                    res.at[0],
-                )[step - 1]
-                arrived(ref, res_recv.at[sem(step)])
             if step == 0:
                 res_copy(half, 0, 0, hh, chunk, -1, RIGHT, sem(1))
                 res_copy(half, 0, 0, hh, chunk, -1, LEFT, sem(1))
@@ -333,7 +333,7 @@
                 res_copy(half, 2, 1, hh, chunk, 1, DOWN, sem(5))
         if step < 3:
             for half in range(2):
-                number = (turn * 5 + (3 if step < 2 else 4) - 1) * 2 + half
+                number = sem(3 if step < 2 else 4)
                 for a in ((0,), (-1, 1), (2,))[step]:
                     res_copy(half, a, 0, hh, chunk, -1, UP, number)
                     res_copy(half, a, 0, hh, chunk, -1, DOWN, number)
@@ -544,7 +544,7 @@
             dma,
             dma((2,)),
             dma,
-            dma((40,)),
+            dma((20,)),
             dma,
             dma((4,)),
             dma((2,)),

time: 80.8 us -> 80.6 us (level)
  no operation moved by 1% of the time
where the time goes in v6:
time: 80.6 us; the launch traced here: 80.4 us
  Pallas kernels  80.4 us (100%)
    pallas_call x1, Pallas kernels, on_device(): pl.pallas_call(kernel, out_shape=jax.ShapeDtypeStruct((SLABS, 1, CELLS),...  79.1 us

profile of v6, /device:TPU:1, one launch (start us, length us, event | category | flops | bytes accessed | tf_op | source)
XLA Modules:
  0.0 80.4 jit_solution(10511165205708195390)
XLA Ops:
  0.0 79.1 %shard_map.55.parts_ref = f32[16,1,512]{2,1,0:T(1,128)} custom-call(s32[1,512]{1,0:T(1,128)} %bitcast.4, s32[1,512]{1,0:T(1,128)} %label_hbm.1, bf16[512,128]{1,0:T(8,128)(2,1)} %bitcast.3, bf16[2,512,512]{2,1,0:T(8,128)(2,1)} %fields_hbm.1, bf16[2,128,512]{2,1,0:T(8,128)(2,1)} %green_hbm.1), custom_call_target="tpu_custom_call" | custom-call | tf_op jit(solution)/shard_map/pallas_call | solution.py:515
  79.1 1.4 %shard_map.56 = f32[1,512]{1,0:T(1,128)} custom-call(f32[16,1,512]{2,1,0:T(1,128)} %shard_map.55.parts_ref), custom_call_target="tpu_custom_call" | custom-call | tf_op jit(solution)/shard_map/pallas_call | solution.py:565
